TPU v7x, 32 devices: a whole 2x2x4 slice. The times are simulated.
32 devices in a mesh: narrow: 4 (over y, x), region: 8 (over z, core).
Axes of the slice: x: 2, y: 2, z: 4, core: 2. Of those that a mesh axis runs over, the one named last changes fastest.
Arguments:
- point_feats: bfloat16 [64, 131072], P(None, ('narrow', 'region')), may hold values from -6 to 6
- point_owner: int32 [131072, 1], P(('narrow', 'region')), may hold values from 0 to 31; in each aligned block of 4096 rows (0 to 4095, 4096 to 8191, ...) at most 256 rows name the same one
- point_voxel: int32 [131072], P(('narrow', 'region')), may hold values from 0 to 12287
- weight: bfloat16 [9, 64, 192], replicated, may hold values from -0.15625 to 0.15625
- cotangent: bfloat16 [64, 192, 2048], P(None, 'region', 'narrow'), may hold values from -6 to 6
Outputs:
- conv_out: bfloat16 [64, 192, 2048], P(None, 'region', 'narrow')
- point_grad: bfloat16 [64, 131072], P(None, ('narrow', 'region'))
- weight_grad: float32 [9, 64, 192], replicated
Inputs may be any that keep to these rules, and one draw needn't show every extreme that they name: `point_owner`: among the 4096 points of one device no owner is named more than 256 times, a bound that some block reaches.
All inputs are finite; a program needn't handle non-finite values.
Results may differ from a plain program's by a relative error of at most 0.0036.
Values may be sent and summed in bfloat16 or wider, within the bound.
A program may use at most 192 MiB of HBM per device.

v0:
```python
import math

import jax
import jax.numpy as jnp
from jax import lax
from jax.sharding import PartitionSpec as P

NZ = 64
CY = 8


def extended(cells, sides, width):
    for axis, dim in sides:
        count = lax.axis_size(axis)
        ends = count - 1
        head = lax.slice_in_dim(cells, 0, width, axis=dim)
        tail = lax.slice_in_dim(cells, cells.shape[dim] - width, cells.shape[dim], axis=dim)
        cells = jnp.concatenate(
            [
                lax.ppermute(tail, axis, [(i, (i + 1) % count) for i in range(ends)]),
                cells,
                lax.ppermute(head, axis, [((i + 1) % count, i) for i in range(ends)]),
            ],
            axis=dim,
        )
    return cells


def stack_depth(padded, offsets, depth):
    return jnp.concatenate([padded[..., o : o + depth] for o in offsets], axis=0)


def shards(point_feats, point_owner, point_voxel, weight, cotangent):
    n_narrow = lax.axis_size("narrow")
    n_region = lax.axis_size("region")
    devices = n_narrow * n_region
    chans, points_here = point_feats.shape
    slots = 2 * points_here // devices
    rows_x = cotangent.shape[1]
    voxels = rows_x * CY * NZ
    owner = point_owner[:, 0]
    marks = (owner[:, None] == jnp.arange(devices, dtype=jnp.int32)[None, :]).astype(jnp.int32)
    slot = jnp.sum(jnp.cumsum(marks, axis=0) * marks, axis=1) - 1
    send_feats = jnp.zeros((devices, slots, chans), jnp.bfloat16).at[owner, slot].set(point_feats.T)
    send_feats = send_feats.reshape(devices, slots * chans)
    send_vox = jnp.zeros((devices, slots), jnp.int32).at[owner, slot].set(point_voxel)
    got_feats, got_vox = (
        lax.all_to_all(send_feats, ("narrow", "region"), split_axis=0, concat_axis=0, tiled=True),
        lax.all_to_all(send_vox, ("narrow", "region"), split_axis=0, concat_axis=0, tiled=True),
    )
    incoming = got_feats.reshape(devices * slots, chans).astype(jnp.float32)
    targets = got_vox.reshape(devices * slots)
    sums = jax.ops.segment_sum(incoming, targets, num_segments=voxels)
    grid = sums.T.astype(jnp.bfloat16).reshape(chans, rows_x, CY, NZ)
    grads = cotangent.reshape(chans, rows_x, CY, NZ)
    padded = extended(grid, (("narrow", 2), ("region", 1)), 1)
    gpad = extended(grads, (("narrow", 2), ("region", 1)), 1)
    padded = jnp.pad(padded, ((0, 0), (0, 0), (0, 0), (1, 1)))
    stacked = stack_depth(padded, [0, 1, 2], NZ)
    gpad = jnp.pad(gpad, ((0, 0), (0, 0), (0, 0), (1, 1)))
    gstack = stack_depth(gpad, [2, 1, 0], NZ)
    flipped = weight.reshape(9, chans, 3, chans).transpose(0, 3, 2, 1).reshape(9, chans, 3 * chans)
    result = jnp.zeros((chans, rows_x, CY, NZ), jnp.float32)
    backward = jnp.zeros((chans, rows_x, CY, NZ), jnp.float32)
    kernels = []
    for a in range(3):
        for b in range(3):
            k = a * 3 + b
            window = stacked[:, a : a + rows_x, b : b + CY]
            result = result + jnp.einsum(
                "ok,kxyz->oxyz", weight[k], window, preferred_element_type=jnp.float32
            )
            kernels.append(
                jnp.einsum("oxyz,kxyz->ok", grads, window, preferred_element_type=jnp.float32)
            )
            backward = backward + jnp.einsum(
                "ck,kxyz->cxyz",
                flipped[k],
                gstack[:, 2 - a : 2 - a + rows_x, 2 - b : 2 - b + CY],
                preferred_element_type=jnp.float32,
            )
    conv_out = result.astype(jnp.bfloat16).reshape(chans, rows_x, CY * NZ)
    total_cells = rows_x * n_region * CY * n_narrow * NZ
    weight_grad = lax.psum(jnp.stack(kernels), ("narrow", "region")) * (
        1.0 / math.sqrt(total_cells)
    )
    grad_flat = backward.astype(jnp.bfloat16).reshape(chans, voxels)
    picked = jnp.take(grad_flat, targets, axis=1).T.reshape(devices, slots * chans)
    returned = lax.all_to_all(picked, ("narrow", "region"), split_axis=0, concat_axis=0, tiled=True)
    returned = returned.reshape(devices, slots, chans)
    point_grad = returned[owner, slot].T
    return (conv_out, point_grad, weight_grad)


def solution(mesh):
    in_specs = (
        P(None, ("narrow", "region")),
        P(("narrow", "region"), None),
        P(("narrow", "region")),
        P(),
        P(None, "region", "narrow"),
    )
    out_specs = (P(None, "region", "narrow"), P(None, ("narrow", "region")), P())
    return jax.shard_map(shards, mesh=mesh, in_specs=in_specs, out_specs=out_specs, check_vma=False)
```

profile of v0, /device:TPU:0, one launch (start us, length us, event | category | flops | bytes accessed | tf_op | source)
XLA Modules:
  0.0 687.0 jit_solution(5900122822803206030)
XLA Ops:
  7.9 9.2 %reduce-window.6 = s32[32,32,128]{2,1,0:T(8,128)S(1)} reduce-window(s32[32,32,128]{2,1,0:T(8,128)S(1)} %fusion.21, s32[]{:T(128)} %constant.14.clone.1), window={size=1x1x128 pad=0_0x0_0x127_0}, to_apply=%region_0.0 | reduce-window | flops 16646144 | bytes 1048580 | tf_op jit(solution)/shard_map/reduce-window
  21.8 16.3 %scatter_custom_fusion.1 = s32[8192]{0:T(1024)} fusion(s32[4096]{0:T(1024)S(1)} %broadcast_select_fusion.1, s32[4096]{0:T(1024)} %param.7, s32[]{:T(128)} %constant.14.clone.1), kind=kCustom, calls=%fused_computation.98 | custom fusion | bytes 33280
  38.1 7.4 %all-to-all-start = ((s32[32,1,256]{2,1,0:T(1,128)}), s32[32,1,256]{2,1,0:T(1,128)}, u32[]{:S(2)}, u32[]{:S(2)}) async-start(s32[32,1,256]{2,1,0:T(1,128)} %bitcast.5), calls=%async_computation | async-start | bytes 65536 | tf_op jit(solution)/shard_map/all_to_all | solution.py:49
  60.9 12.9 %scatter_custom_fusion.2 = bf16[8192,64]{1,0:T(8,128)(2,1)} fusion(s32[4096]{0:T(1024)} %copy-done.17, bf16[4096,64]{1,0:T(8,128)(2,1)} %copy.54, bf16[]{:T(256)} %constant.33.clone.1), kind=kCustom, calls=%fused_computation.45 | custom fusion | bytes 1049088
  73.8 6.2 all_to_all.24
  80.6 9.4 %reduce.11 = bf16[32,16384]{1,0:T(8,128)(2,1)} reduce(bf16[32,1,16384]{2,1,0:T(2,128)(2,1)} %all_to_all.24, bf16[]{:T(256)} %broadcast.231), dimensions={1}, to_apply=%all_to_all.24.reduce_sub_computation | reduce | bytes 2097154 | tf_op jit(solution)/shard_map/all_to_all | solution.py:48
  106.1 7.6 %all-to-all-start.1 = ((bf16[32,2,8192]{2,1,0:T(2,128)(2,1)}), bf16[32,2,8192]{2,1,0:T(2,128)(2,1)}, u32[]{:S(2)}, u32[]{:S(2)}) async-start(bf16[32,2,8192]{2,1,0:T(2,128)(2,1)} %reshape.224), calls=%async_computation.1 | async-start | bytes 2097152 | tf_op jit(solution)/shard_map/all_to_all | solution.py:48
  122.4 9.0 %select_maximum_fusion = bf16[64,26,10,66]{0,3,2,1:T(8,128)(2,1)S(1)} fusion(bf16[64,1,10,64]{0,3,2,1:T(8,128)(2,1)S(1)} %collective-permute-done.7, bf16[64,1,10,64]{0,3,2,1:T(8,128)(2,1)S(1)} %collective-permute-done.6, bf16[64,24,1,64]{0,3,2,1:T(8,128)(2,1)} %collective-permute-done.5, bf16[64,24,8,64]{0,3,2,1:T(8,128)(2,1)S(1)} %bitcast.265, ...), kind=kLoop, calls=%fused_computation.12 | loop fusion | flops 19768320 | bytes 4326400 | tf_op jit(solution)/shard_map/concatenate | solution.py:18
  133.8 11.6 %pad_maximum_fusion.1 = bf16[192,26,10,64]{0,3,2,1:T(8,128)(2,1)S(1)} fusion(bf16[64,26,10,64]{0,3,2,1:T(8,128)(2,1)S(1)} %get-tuple-element.15, bf16[64,1,10,64]{0,3,2,1:T(8,128)(2,1)S(1)} %collective-permute-done.7, bf16[64,24,1,64]{0,3,2,1:T(8,128)(2,1)} %collective-permute-done.5, bf16[64,24,8,64]{0,3,2,1:T(8,128)(2,1)S(1)} %bitcast.266, ...), kind=kLoop, calls=%fused_computation.9 | loop fusion | flops 44728320 | bytes 12779520 | tf_op jit(solution)/shard_map/concatenate | solution.py:30
  181.2 18.4 %add_convert_fusion = bf16[24,8,64,64]{3,2,1,0:T(8,128)(2,1)} fusion(f32[24,8,64,64]{3,2,1,0:T(8,128)} %fusion.62, f32[24,8,64,64]{3,2,1,0:T(8,128)} %fusion.61, f32[24,8,64,64]{3,2,1,0:T(8,128)} %fusion.60, f32[24,8,64,64]{3,2,1,0:T(8,128)} %fusion.59, f32[24,8,64,64]{3,2,1,0:T(8,128)} %fusion.58, f32[24,8,64,64]{3,2,1,0:T(8,128)} %fusion.57, ...), kind=kOutput, calls=%fused_computation.10 | convolution fusion | flops 309067776 | bytes 33153024 | tf_op jit(solution)/shard_map/ck,kxyz->cxyz/dot_general | solution.py:76
  199.6 30.4 %gather_fusion = bf16[8192,64]{1,0:T(8,128)(2,1)} fusion(bf16[64,12288]{0,1:T(8,128)(2,1)} %bitcast.281, s32[8192]{0:T(1024)S(1)} %copy-done.15), kind=kCustom, calls=%fused_computation | custom fusion | bytes 2129920 | tf_op jit(solution)/shard_map/jit(_take)/gather | solution.py:88
  230.1 6.6 broadcast_select_fusion
  242.8 9.4 %reduce.12 = bf16[32,16384]{1,0:T(8,128)(2,1)} reduce(bf16[32,1,16384]{2,1,0:T(2,128)(2,1)} %all_to_all.25, bf16[]{:T(256)} %broadcast.231), dimensions={1}, to_apply=%all_to_all.25.reduce_sub_computation | reduce | bytes 2097154 | tf_op jit(solution)/shard_map/all_to_all | solution.py:89
  254.8 21.9 %all-to-all-start.2 = ((bf16[32,2,8192]{2,1,0:T(2,128)(2,1)}), bf16[32,2,8192]{2,1,0:T(2,128)(2,1)}, u32[]{:S(2)}, u32[]{:S(2)}) async-start(bf16[32,2,8192]{2,1,0:T(2,128)(2,1)} %reshape.226), calls=%async_computation.2 | async-start | bytes 2097152 | tf_op jit(solution)/shard_map/all_to_all | solution.py:89
  282.7 9.0 %convert_reduce_fusion = f32[32,16384]{1,0:T(8,128)} fusion(bf16[32,1,16384]{2,1,0:T(2,128)(2,1)} %reshape.225), kind=kLoop, calls=%fused_computation.25 | loop fusion | flops 524288 | bytes 3145728 | tf_op jit(solution)/shard_map/convert_element_type | solution.py:51
  296.0 49.3 %scatter_custom_fusion = f32[12288,64]{1,0:T(8,128)} fusion(s32[8192]{0:T(1024)} %bitcast.6, f32[8192,64]{1,0:T(8,128)} %reshape.171, f32[]{:T(128)} %constant.13.clone.1), kind=kCustom, calls=%fused_computation.23 | custom fusion | flops 524288 | bytes 3146240 | tf_op jit(solution)/shard_map/scatter-add | solution.py:53
  348.4 9.9 %collective-permute-start = (bf16[64,24,1,64]{0,3,2,1:T(8,128)(2,1)S(1)}, bf16[64,24,1,64]{0,3,2,1:T(8,128)(2,1)S(1)}, u32[]{:S(2)}, u32[]{:S(2)}) collective-permute-start(bf16[64,24,1,64]{0,3,2,1:T(8,128)(2,1)S(1)} %get-tuple-element.24), channel_id=1, source_target_pairs={{0,8},{8,16},{16,24},{1,9},{9,17},{17,25},{2,10},{10,18},{18,26},{... | collective-permute-start | bytes 589832 | tf_op jit(solution)/shard_map/ppermute | solution.py:20
  365.8 7.8 %collective-permute-done.1 = bf16[64,24,1,64]{0,3,2,1:T(8,128)(2,1)S(1)} collective-permute-done((bf16[64,24,1,64]{0,3,2,1:T(8,128)(2,1)S(1)}, bf16[64,24,1,64]{0,3,2,1:T(8,128)(2,1)S(1)}, u32[]{:S(2)}, u32[]{:S(2)}) %collective-permute-start.1) | collective-permute-done | bytes 196640 | tf_op jit(solution)/shard_map/ppermute | solution.py:22
  384.0 8.7 %reduce.6 = bf16[32,16384]{1,0:T(8,128)(2,1)} reduce(bf16[32,1,16384]{2,1,0:T(2,128)(2,1)} %reshape.227, bf16[]{:T(256)} %constant.72), dimensions={1}, to_apply=%all_to_all.23.reduce_sub_computation | reduce | bytes 2097154 | tf_op jit(solution)/shard_map/all_to_all | solution.py:89
  396.8 67.3 %gather_fusion.1 = bf16[4096,64]{1,0:T(8,128)(2,1)} fusion(bf16[32,256,64]{2,1,0:T(8,128)(2,1)} %reshape.141, s32[4096]{0:T(1024)S(1)} %bitcast.276), kind=kCustom, calls=%fused_computation.1 | custom fusion | bytes 1081344 | tf_op jit(solution)/shard_map/gather | solution.py:91
  466.4 9.6 %select_maximum_fusion.4 = bf16[64,26,10,66]{0,3,2,1:T(8,128)(2,1)S(1)} fusion(bf16[64,1,10,64]{0,3,2,1:T(8,128)(2,1)} %collective-permute-done.3, bf16[64,1,10,64]{0,3,2,1:T(8,128)(2,1)} %collective-permute-done.2, bf16[64,24,1,64]{0,3,2,1:T(8,128)(2,1)} %copy-done.3, bf16[64,24,8,64]{0,3,2,1:T(8,128)(2,1)} %bitcast.279, ...), kind=kLoop, calls=%fused_computation.16 | loop fusion | flops 19768320 | bytes 4326400 | tf_op jit(solution)/shard_map/concatenate | solution.py:18
  478.4 11.3 %pad_maximum_fusion = bf16[192,26,10,64]{0,3,2,1:T(8,128)(2,1)S(1)} fusion(bf16[64,26,10,64]{0,3,2,1:T(8,128)(2,1)S(1)} %get-tuple-element.17, bf16[64,1,10,64]{0,3,2,1:T(8,128)(2,1)} %collective-permute-done.3, bf16[64,24,1,64]{0,3,2,1:T(8,128)(2,1)S(1)} %copy-done.4, bf16[64,24,8,64]{0,3,2,1:T(8,128)(2,1)S(1)} %bitcast.280, ...), kind=kLoop, calls=%fused_computation.8 | loop fusion | flops 44728320 | bytes 12779520 | tf_op jit(solution)/shard_map/concatenate | solution.py:30
  544.8 18.6 %add_convert_fusion.1 = bf16[24,8,64,64]{3,2,1,0:T(8,128)(2,1)S(1)} fusion(f32[24,8,64,64]{3,2,1,0:T(8,128)} %fusion.23, f32[24,8,64,64]{3,2,1,0:T(8,128)} %fusion.25, f32[24,8,64,64]{3,2,1,0:T(8,128)} %fusion.27, f32[24,8,64,64]{3,2,1,0:T(8,128)} %fusion.29, f32[24,8,64,64]{3,2,1,0:T(8,128)} %fusion.31, f32[24,8,64,64]{3,2,1,0:T(8,128)} %fusion.33, ...), kind=kOutput, calls=%fused_computation.11 | convolution fusion | flops 309067776 | bytes 33161216 | tf_op jit(solution)/shard_map/ok,kxyz->oxyz/dot_general | solution.py:70
  566.5 111.5 %all-reduce.4.cloned.1.call-done = f32[9,64,192]{2,1,0:T(8,128)} async-done(((f32[9,64,192]{2,1,0:T(8,128)}), f32[9,64,192]{2,1,0:T(8,128)}) %all-reduce.4.cloned.1.call-update) | async-done | bytes 442384 | tf_op jit(solution)/shard_map/psum | solution.py:84
  (124 shorter events, 193.1 us)
Async XLA Ops:
  21.8 16.3 %copy-start.17 = (s32[4096]{0:T(1024)}, s32[4096]{0:T(1024)S(1)}, u32[]{:S(2)}) copy-start(s32[4096]{0:T(1024)S(1)} %broadcast_select_fusion.1) | copy-start | bytes 49156
  38.1 68.0 %all-to-all-start = ((s32[32,1,256]{2,1,0:T(1,128)}), s32[32,1,256]{2,1,0:T(1,128)}, u32[]{:S(2)}, u32[]{:S(2)}) async-start(s32[32,1,256]{2,1,0:T(1,128)} %bitcast.5), calls=%async_computation | async-start | bytes 65536 | tf_op jit(solution)/shard_map/all_to_all | solution.py:49
  49.9 65.2 %collective-permute-start.4 = (bf16[64,24,1,64]{0,3,2,1:T(8,128)(2,1)}, bf16[64,24,1,64]{0,3,2,1:T(8,128)(2,1)S(1)}, u32[]{:S(2)}, u32[]{:S(2)}) collective-permute-start(bf16[64,24,1,64]{0,3,2,1:T(8,128)(2,1)} %get-tuple-element.22), channel_id=1, source_target_pairs={{0,8},{8,16},{16,24},{1,9},{9,17},{17,25},{2,10},{10,18},{18,26},{... | collective-permute-start | bytes 589832 | tf_op jit(solution)/shard_map/ppermute | solution.py:20
  53.5 61.6 %collective-permute-start.5 = (bf16[64,24,1,64]{0,3,2,1:T(8,128)(2,1)}, bf16[64,24,1,64]{0,3,2,1:T(8,128)(2,1)}, u32[]{:S(2)}, u32[]{:S(2)}) collective-permute-start(bf16[64,24,1,64]{0,3,2,1:T(8,128)(2,1)} %get-tuple-element.23), channel_id=1, source_target_pairs={{8,0},{16,8},{24,16},{9,1},{17,9},{25,17},{10,2},{18,10},{26,18},{... | collective-permute-start | bytes 589832 | tf_op jit(solution)/shard_map/ppermute | solution.py:22
  106.1 148.8 %all-to-all-start.1 = ((bf16[32,2,8192]{2,1,0:T(2,128)(2,1)}), bf16[32,2,8192]{2,1,0:T(2,128)(2,1)}, u32[]{:S(2)}, u32[]{:S(2)}) async-start(bf16[32,2,8192]{2,1,0:T(2,128)(2,1)} %reshape.224), calls=%async_computation.1 | async-start | bytes 2097152 | tf_op jit(solution)/shard_map/all_to_all | solution.py:48
  115.9 4.8 collective-permute-start.6
  118.0 4.4 collective-permute-start.7
  133.7 11.6 %copy-start.7 = (bf16[1,64,3,64]{1,3,2,0:T(8,128)(2,1)S(1)}, bf16[1,64,3,64]{1,3,2,0:T(8,128)(2,1)}, u32[]{:S(2)}) copy-start(bf16[1,64,3,64]{1,3,2,0:T(8,128)(2,1)} %copy.58) | copy-start | bytes 73732
  145.4 4.5 copy-start.8
  149.8 4.4 copy-start.9
  158.6 4.4 copy-start.11
  163.0 4.5 copy-start.12
  171.9 4.4 copy-start.14
  176.3 4.9 copy-start.6
  181.2 18.4 %copy-start.15 = (s32[8192]{0:T(1024)S(1)}, s32[8192]{0:T(1024)}, u32[]{:S(2)}) copy-start(s32[8192]{0:T(1024)} %broadcast_clamp_fusion) | copy-start | bytes 98308
  199.6 30.4 %copy-start.16 = (pred[8192]{0:T(1024)(128)(4,1)S(1)}, pred[8192]{0:T(1024)(128)(4,1)}, u32[]{:S(2)}) copy-start(pred[8192]{0:T(1024)(128)(4,1)} %compare_and_fusion) | copy-start | bytes 24580
  254.8 123.0 %all-to-all-start.2 = ((bf16[32,2,8192]{2,1,0:T(2,128)(2,1)}), bf16[32,2,8192]{2,1,0:T(2,128)(2,1)}, u32[]{:S(2)}, u32[]{:S(2)}) async-start(bf16[32,2,8192]{2,1,0:T(2,128)(2,1)} %reshape.226), calls=%async_computation.2 | async-start | bytes 2097152 | tf_op jit(solution)/shard_map/all_to_all | solution.py:89
  276.8 401.3 %all-reduce.4.cloned.1.call-start = ((), (), s32[]{:S(2)}) async-start(), calls=%async_computation.3 | async-start | bytes 1179648 | tf_op jit(solution)/shard_map/psum | solution.py:84
  348.3 25.3 %copy-start.1 = (bf16[12288,64]{1,0:T(8,128)(2,1)}, bf16[12288,64]{1,0:T(8,128)(2,1)S(1)}, u32[]{:S(2)}) copy-start(bf16[12288,64]{1,0:T(8,128)(2,1)S(1)} %convert_element_type.29) | copy-start | bytes 4718596
  348.4 17.4 %collective-permute-start = (bf16[64,24,1,64]{0,3,2,1:T(8,128)(2,1)S(1)}, bf16[64,24,1,64]{0,3,2,1:T(8,128)(2,1)S(1)}, u32[]{:S(2)}, u32[]{:S(2)}) collective-permute-start(bf16[64,24,1,64]{0,3,2,1:T(8,128)(2,1)S(1)} %get-tuple-element.24), channel_id=1, source_target_pairs={{0,8},{8,16},{16,24},{1,9},{9,17},{17,25},{2,10},{10,18},{18,26},{... | collective-permute-start | bytes 589832 | tf_op jit(solution)/shard_map/ppermute | solution.py:20
  358.4 15.3 %collective-permute-start.1 = (bf16[64,24,1,64]{0,3,2,1:T(8,128)(2,1)S(1)}, bf16[64,24,1,64]{0,3,2,1:T(8,128)(2,1)S(1)}, u32[]{:S(2)}, u32[]{:S(2)}) collective-permute-start(bf16[64,24,1,64]{0,3,2,1:T(8,128)(2,1)S(1)} %get-tuple-element.25), channel_id=1, source_target_pairs={{8,0},{16,8},{24,16},{9,1},{17,9},{25,17},{10,2},{18,10},{26,18},{... | collective-permute-start | bytes 589832 | tf_op jit(solution)/shard_map/ppermute | solution.py:22
  374.5 91.9 %collective-permute-start.2 = (bf16[64,1,10,64]{0,3,2,1:T(8,128)(2,1)}, bf16[64,1,10,64]{0,3,2,1:T(8,128)(2,1)}, u32[]{:S(2)}, u32[]{:S(2)}) collective-permute-start(bf16[64,1,10,64]{0,3,2,1:T(8,128)(2,1)} %get-tuple-element.20), channel_id=1, source_target_pairs={{0,1},{1,2},{2,3},{3,4},{4,5},{5,6},{6,7},{8,9},{9,10},{10,11},{11... | collective-permute-start | bytes 245768 | tf_op jit(solution)/shard_map/ppermute | solution.py:20
  376.5 89.9 %collective-permute-start.3 = (bf16[64,1,10,64]{0,3,2,1:T(8,128)(2,1)}, bf16[64,1,10,64]{0,3,2,1:T(8,128)(2,1)}, u32[]{:S(2)}, u32[]{:S(2)}) collective-permute-start(bf16[64,1,10,64]{0,3,2,1:T(8,128)(2,1)} %get-tuple-element.21), channel_id=1, source_target_pairs={{1,0},{2,1},{3,2},{4,3},{5,4},{6,5},{7,6},{9,8},{10,9},{11,10},{12... | collective-permute-start | bytes 245768 | tf_op jit(solution)/shard_map/ppermute | solution.py:22
  489.7 53.0 %copy-start = (bf16[192,26,10,64]{0,3,2,1:T(8,128)(2,1)}, bf16[192,26,10,64]{0,3,2,1:T(8,128)(2,1)S(1)}, u32[]{:S(2)}) copy-start(bf16[192,26,10,64]{0,3,2,1:T(8,128)(2,1)S(1)} %pad_maximum_fusion) | copy-start | bytes 19169284
  (6 other events, 17.1 us)
Sparse Core Ops, SparseCore 0:
  544.9 133.0 all-reduce.3
where the time goes:
time: 695 us; the launch traced here: 687 us
  local copies, waits for them, and re-layouts  201 us (29%)
  other arithmetic  157 us (23%)
  matrix products  128 us (18%)
  waiting for transfers between devices  127 us (18%)
  starting transfers between devices  59.7 us (9%)
  between operations  14.6 us (2%)
    psum x1, waiting for transfers between devices, shards(): lax.psum(jnp.stack(kernels), ('narrow', 'region'))  112 us
    gather x1, local copies, waits for them, and re-layouts, shards(): point_grad = returned[owner, slot].T  67.3 us
    unnamed x46, local copies, waits for them, and re-layouts  57.5 us
    dot_general x9, matrix products, shards(): jnp.einsum('ck,kxyz->cxyz', flipped[k], gstack[:, 2 - a:2 - a + rows_x, 2...  54.2 us
    dot_general x9, matrix products, shards(): jnp.einsum('ok,kxyz->oxyz', weight[k], window, preferred_element_type=jnp...  53.8 us
    scatter-add x1, other arithmetic, shards(): sums = jax.ops.segment_sum(incoming, targets, num_segments=voxels)  49.3 us
    gather x1, local copies, waits for them, and re-layouts, shards(): jnp.take(grad_flat, targets, axis=1).T.reshape(devices, slots * chans)  30.4 us
    concatenate x2, other arithmetic, stack_depth(): return jnp.concatenate([padded[..., o:o + depth] for o in offsets], axis=0)  22.9 us
  transfers between devices with their start and end apart: 12, of which 4 were waited for; matrix products, arithmetic and copies ran while one was open for 53% of the time, Pallas kernels for 0%

commit v1 on v0

v1 whole, which is shorter than its diff:
```python
import functools
import math

import jax
import jax.numpy as jnp
from jax import lax
from jax.experimental import pallas as pl
from jax.experimental.pallas import tpu as pltpu
from jax.sharding import PartitionSpec as P

NZ = 64
CY = 8
AXES = ("narrow", "region")
GROUP = 8
TILE = 512


def extended(cells, sides):
    for axis, dim in sides:
        count = lax.axis_size(axis)
        ends = count - 1
        head = lax.slice_in_dim(cells, 0, 1, axis=dim)
        tail = lax.slice_in_dim(cells, cells.shape[dim] - 1, cells.shape[dim], axis=dim)
        cells = jnp.concatenate(
            [
                lax.ppermute(tail, axis, [(i, (i + 1) % count) for i in range(ends)]),
                cells,
                lax.ppermute(head, axis, [((i + 1) % count, i) for i in range(ends)]),
            ],
            axis=dim,
        )
    return cells


def stacked_depth(cells):
    padded = extended(cells, (("narrow", 1), ("region", 0)))
    padded = jnp.pad(padded, ((0, 0), (0, 0), (1, 1), (0, 0)))
    return jnp.concatenate([padded[:, :, d : d + NZ] for d in range(3)], axis=3)


def convolved(stack, kernel):
    return lax.conv_general_dilated(
        stack,
        kernel,
        (1, 1),
        "VALID",
        dimension_numbers=lax.ConvDimensionNumbers((2, 3, 0, 1), (3, 2, 0, 1), (2, 3, 0, 1)),
        preferred_element_type=jnp.float32,
    )


def packed(buf, out_ref):
    rows = out_ref.shape[0]

    def tile(t, _):
        low = pl.multiple_of(t * TILE, TILE)
        left = buf[pl.ds(low, TILE), :]
        right = buf[pl.ds(rows + low, TILE), :]
        out_ref[pl.ds(low, TILE), :] = jnp.concatenate([left, right], axis=1).astype(jnp.bfloat16)

    lax.fori_loop(0, rows // TILE, tile, None)


def unpacked(in_ref, buf):
    rows, lanes = in_ref.shape

    def tile(t, _):
        low = pl.multiple_of(t * TILE, TILE)
        both = in_ref[pl.ds(low, TILE), :].astype(jnp.float32)
        buf[pl.ds(low, TILE), :] = both[:, : lanes // 2]
        buf[pl.ds(rows + low, TILE), :] = both[:, lanes // 2 :]

    lax.fori_loop(0, rows // TILE, tile, None)


def each_arrival(devices, slots, rows, count_ref, visit):
    half = slots // 2

    def source(s, _):
        here = count_ref[s]
        for h in range(2):
            some = jnp.clip(here - h * half, 0, half)

            def group(j, _):
                for u in range(GROUP):
                    r = j * GROUP + u
                    visit(u, s * slots + h * half + r, h * rows + s * half + r)

            lax.fori_loop(0, (some + GROUP - 1) // GROUP, group, None)

    lax.fori_loop(0, devices, source, None)


def place_kernel(place_ref, vox_ref, rows_ref, out_ref, vox_out_ref, buf):
    def group(j, _):
        for u in range(GROUP):
            p = j * GROUP + u
            d = place_ref[p]
            buf[pl.ds(d, 1), :] = rows_ref[pl.ds(p, 1), :]
            vox_out_ref[d] = vox_ref[p]

    lax.fori_loop(0, rows_ref.shape[0] // GROUP, group, None)
    packed(buf, out_ref)


def splat_kernel(devices, slots, vox_ref, count_ref, got_ref, grid_ref, buf, *sums):
    unpacked(got_ref, buf)
    voxels, chans = grid_ref.shape

    def clear(t, _):
        for each in sums:
            each[pl.ds(pl.multiple_of(t * TILE, TILE), TILE), :] = jnp.zeros((TILE, chans), jnp.float32)

    lax.fori_loop(0, voxels // TILE, clear, None)

    def visit(u, k, r):
        v = vox_ref[k]
        each = sums[u % len(sums)]
        each[pl.ds(v, 1), :] += buf[pl.ds(r, 1), :]

    each_arrival(devices, slots, got_ref.shape[0], count_ref, visit)

    def finish(t, _):
        at = pl.ds(pl.multiple_of(t * TILE, TILE), TILE)
        total = sums[0][at, :]
        for each in sums[1:]:
            total += each[at, :]
        grid_ref[at, :] = total.astype(jnp.bfloat16)

    lax.fori_loop(0, voxels // TILE, finish, None)


def pick_kernel(devices, slots, vox_ref, count_ref, table_ref, out_ref, buf):
    def visit(u, k, r):
        buf[pl.ds(r, 1), :] = table_ref[pl.ds(vox_ref[k], 1), :]

    each_arrival(devices, slots, out_ref.shape[0], count_ref, visit)
    packed(buf, out_ref)


def collect_kernel(place_ref, back_ref, out_ref, buf):
    unpacked(back_ref, buf)

    def group(j, _):
        for u in range(GROUP):
            p = j * GROUP + u
            out_ref[pl.ds(p, 1), :] = buf[pl.ds(place_ref[p], 1), :]

    lax.fori_loop(0, out_ref.shape[0] // GROUP, group, None)


def call(kernel, out_shape, kinds, out_kinds, scratch, cost, *operands):
    where = {"s": pltpu.SMEM, "v": pltpu.VMEM}
    specs = [pl.BlockSpec(memory_space=where[k]) for k in out_kinds]
    return pl.pallas_call(
        kernel,
        out_shape=out_shape,
        in_specs=[pl.BlockSpec(memory_space=where[k]) for k in kinds],
        out_specs=specs if len(specs) > 1 else specs[0],
        scratch_shapes=scratch,
        compiler_params=pltpu.CompilerParams(vmem_limit_bytes=50 << 20),
        cost_estimate=pl.CostEstimate(flops=0, bytes_accessed=cost, transcendentals=0),
    )(*operands)


def ranks(owner, devices):
    span = 128
    chunks = owner.shape[0] // span
    marks = owner.reshape(chunks, span)[:, :, None] == jnp.arange(devices, dtype=jnp.int32)
    ones = marks.astype(jnp.bfloat16)
    before = (jnp.arange(span)[:, None] > jnp.arange(span)[None, :]).astype(jnp.bfloat16)
    inner = jnp.einsum("ij,cjo->cio", before, ones, preferred_element_type=jnp.float32)
    tallies = jnp.sum(ones.astype(jnp.float32), axis=1)
    ahead = (jnp.arange(chunks)[:, None] > jnp.arange(chunks)[None, :]).astype(jnp.bfloat16)
    starts = jnp.einsum("ij,jo->io", ahead, tallies.astype(jnp.bfloat16), preferred_element_type=jnp.float32)
    slot = jnp.sum(jnp.where(marks, inner + starts[:, None, :], 0.0), axis=2)
    return slot.reshape(-1).astype(jnp.int32), jnp.sum(tallies, axis=0).astype(jnp.int32)


def exchanged(x):
    return lax.all_to_all(x, AXES, split_axis=0, concat_axis=0, tiled=True)


def shards(point_feats, point_owner, point_voxel, weight, cotangent):
    n_narrow = lax.axis_size("narrow")
    n_region = lax.axis_size("region")
    devices = n_narrow * n_region
    chans, points_here = point_feats.shape
    slots = 2 * points_here // devices
    half = slots // 2
    rows = devices * half
    rows_x = cotangent.shape[1]
    voxels = rows_x * CY * NZ
    f32, bf16, i32 = jnp.float32, jnp.bfloat16, jnp.int32
    buffer = pltpu.VMEM((2 * rows, chans), f32)
    pairs = jax.ShapeDtypeStruct((rows, 2 * chans), bf16)

    owner = point_owner[:, 0]
    slot, sent = ranks(owner, devices)
    place = (slot // half) * rows + owner * half + slot % half
    send, send_vox = call(
        place_kernel,
        (pairs, jax.ShapeDtypeStruct((2 * rows,), i32)),
        "ssv",
        "vs",
        [buffer],
        40 << 20,
        place,
        point_voxel,
        point_feats.T.astype(f32),
    )
    send_vox = send_vox.reshape(2, devices, half).transpose(1, 0, 2).reshape(devices, slots)
    filled = jnp.arange(slots, dtype=i32)[None, :] < sent[:, None]
    got_vox = exchanged(jnp.where(filled, send_vox, voxels))
    got = exchanged(send.reshape(devices, half, 2 * chans)).reshape(rows, 2 * chans)
    count = jnp.sum((got_vox < voxels).astype(i32), axis=1)
    add_at = got_vox.reshape(-1)
    pick_at = jnp.where(got_vox < voxels, got_vox, 0).reshape(-1)

    w = weight.reshape(3, 3, chans, 3, chans)
    backward = w[::-1, ::-1, :, ::-1, :].transpose(0, 1, 3, 2, 4).reshape(3, 3, 3 * chans, chans)
    forward = weight.reshape(3, 3, chans, 3 * chans).transpose(0, 1, 3, 2)

    grads = cotangent.reshape(chans, rows_x, CY, NZ).transpose(1, 2, 3, 0)
    table = convolved(stacked_depth(grads), backward).reshape(voxels, chans)
    picked = call(
        functools.partial(pick_kernel, devices, slots),
        pairs,
        "ssv",
        "v",
        [buffer],
        40 << 20,
        pick_at,
        count,
        table,
    )
    back = exchanged(picked.reshape(devices, half, 2 * chans)).reshape(rows, 2 * chans)

    grid = call(
        functools.partial(splat_kernel, devices, slots),
        jax.ShapeDtypeStruct((voxels, chans), bf16),
        "ssv",
        "v",
        [buffer] + [pltpu.VMEM((voxels + 8, chans), f32)] * 4,
        80 << 20,
        add_at,
        count,
        got,
    )
    stack = stacked_depth(grid.reshape(rows_x, CY, NZ, chans))
    flat = cotangent.reshape(chans, voxels)
    kernels = []
    for a in range(3):
        for b in range(3):
            window = stack[a : a + rows_x, b : b + CY].reshape(voxels, 3 * chans)
            kernels.append(jnp.einsum("ov,vk->ok", flat, window, preferred_element_type=f32))
    total_cells = rows_x * n_region * CY * n_narrow * NZ
    parts = exchanged(jnp.stack(kernels).reshape(devices, -1))
    mine = jnp.sum(parts, axis=0) * (1.0 / math.sqrt(total_cells))
    weight_grad = lax.all_gather(mine, AXES, tiled=True).reshape(9, chans, 3 * chans)

    result = convolved(stack, forward).astype(bf16)
    conv_out = result.transpose(3, 0, 1, 2).reshape(chans, rows_x, CY * NZ)

    point_rows = call(
        collect_kernel,
        jax.ShapeDtypeStruct((points_here, chans), f32),
        "sv",
        "v",
        [buffer],
        40 << 20,
        place,
        back,
    )
    return (conv_out, point_rows.T.astype(bf16), weight_grad)


def solution(mesh):
    in_specs = (
        P(None, AXES),
        P(AXES, None),
        P(AXES),
        P(),
        P(None, "region", "narrow"),
    )
    out_specs = (P(None, "region", "narrow"), P(None, AXES), P())
    return jax.shard_map(shards, mesh=mesh, in_specs=in_specs, out_specs=out_specs, check_vma=False)
```

time: 695 us -> 342 us (0.49); the launches traced: 687 us -> 346 us
  local copies, waits for them, and re-layouts: 201 us -> 71.1 us
  other arithmetic: 157 us -> 36.6 us
  waiting for transfers between devices: 127 us -> 23.4 us
  matrix products: 128 us -> 52.1 us
  Pallas kernels: 0 us -> 54.3 us
  blocking collectives: 0 us -> 43.2 us
  between operations: 14.6 us -> 1.23 us
    dot_general x27 -> x11, matrix products: 128 us -> 14.6 us  [the longest x9 13.4 us: shards(): jnp.einsum('ov,vk->ok', flat, window, preferred_element_type=f32)]
    psum x1 -> x0, waiting for transfers between devices: 112 us -> none  [shards(): lax.psum(jnp.stack(kernels), ('narrow', 'region'))]
    gather x2 -> x0, local copies, waits for them, and re-layouts: 97.8 us -> none  [the longest x1 67.3 us: shards(): point_grad = returned[owner, slot].T]
    pallas_call x0 -> x4, Pallas kernels: none -> 54.3 us  [call(): pl.pallas_call(kernel, out_shape=out_shape, in_specs=[pl.BlockSpec(memory...]
    scatter-add x1 -> x0, other arithmetic: 49.3 us -> none  [shards(): sums = jax.ops.segment_sum(incoming, targets, num_segments=voxels)]
    all_gather x0 -> x1, blocking collectives: none -> 43.2 us  [shards(): lax.all_gather(mine, AXES, tiled=True).reshape(9, chans, 3 * chans)]
    unnamed x46 -> x58, local copies, waits for them, and re-layouts: 57.5 us -> 18.8 us
    conv_general_dilated x0 -> x2, matrix products: none -> 37.5 us  [convolved(): lax.conv_general_dilated(stack, kernel, (1, 1), 'VALID', dimension_number...]
  transfers between devices with their start and end apart: 12 -> 12, of which waited for: 4 -> 4; matrix products, arithmetic and copies ran while one was open for 53% -> 20% of each run, Pallas kernels for 0% -> 13%
where the time goes in v1:
time: 342 us; the launch traced here: 346 us
  local copies, waits for them, and re-layouts  71.1 us (21%)
  starting transfers between devices  64 us (19%)
  Pallas kernels  54.3 us (16%)
  matrix products  52.1 us (15%)
  blocking collectives  43.2 us (13%)
  other arithmetic  36.6 us (11%)
  waiting for transfers between devices  23.4 us (7%)
    pallas_call x4, Pallas kernels, call(): pl.pallas_call(kernel, out_shape=out_shape, in_specs=[pl.BlockSpec(memory...  54.3 us
    all_gather x1, blocking collectives, shards(): lax.all_gather(mine, AXES, tiled=True).reshape(9, chans, 3 * chans)  43.2 us
    all_to_all x4, starting transfers between devices, exchanged(): return lax.all_to_all(x, AXES, split_axis=0, concat_axis=0, tiled=True)  43.1 us
    conv_general_dilated x2, matrix products, convolved(): lax.conv_general_dilated(stack, kernel, (1, 1), 'VALID', dimension_number...  37.5 us
    slice x1, local copies, waits for them, and re-layouts, shards(): window = stack[a:a + rows_x, b:b + CY].reshape(voxels, 3 * chans)  37.2 us
    ppermute x4, waiting for transfers between devices, extended(): lax.ppermute(head, axis, [((i + 1) % count, i) for i in range(ends)])  21.3 us
    unnamed x58, local copies, waits for them, and re-layouts  18.8 us
    concatenate x2, other arithmetic, extended(): jnp.concatenate([lax.ppermute(tail, axis, [(i, (i + 1) % count) for i in...  18.1 us
  transfers between devices with their start and end apart: 12, of which 4 were waited for; matrix products, arithmetic and copies ran while one was open for 20% of the time, Pallas kernels for 13%

profile of v1, /device:TPU:0, one launch (start us, length us, event | category | flops | bytes accessed | tf_op | source)
XLA Modules:
  0.0 346.0 jit_solution(754982748489341450)
XLA Ops:
  6.6 10.7 %shard_map.76 = (bf16[4096,128]{1,0:T(8,128)(2,1)}, s32[8192]{0:T(1024)S(1)}) custom-call(s32[4096]{0:T(1024)S(1)} %fusion.40.place_ref, s32[4096]{0:T(1024)S(1)} %copy-done, f32[4096,64]{1,0:T(8,128)S(1)} %bitcast.140), custom_call_target="tpu_custom_call" | custom-call | bytes 41943040 | tf_op jit(solution)/shard_map/pallas_call | solution.py:155
  18.2 7.3 %all-to-all-start = ((s32[32,1,256]{2,1,0:T(1,128)}), s32[32,1,256]{2,1,0:T(1,128)S(1)}, u32[]{:S(2)}, u32[]{:S(2)}) async-start(s32[32,1,256]{2,1,0:T(1,128)} %copy.38), calls=%async_computation | async-start | bytes 65536 | tf_op jit(solution)/shard_map/all_to_all | solution.py:181
  25.5 3.4 copy.40
  29.9 4.4 %collective-permute-start.4 = (bf16[24,1,64,64]{3,2,1,0:T(8,128)(2,1)}, bf16[24,1,64,64]{3,2,1,0:T(8,128)(2,1)}, u32[]{:S(2)}, u32[]{:S(2)}) collective-permute-start(bf16[24,1,64,64]{3,2,1,0:T(8,128)(2,1)} %get-tuple-element.39), channel_id=1, source_target_pairs={{0,8},{8,16},{16,24},{1,9},{9,17},{17,25},{2,10},{10,18},{18,26},{... | collective-permute-start | bytes 589832 | tf_op jit(solution)/shard_map/ppermute | solution.py:26
  40.4 6.7 %all-to-all-start.1 = ((bf16[32,128,128]{2,1,0:T(8,128)(2,1)}), bf16[32,128,128]{2,1,0:T(8,128)(2,1)S(1)}, u32[]{:S(2)}, u32[]{:S(2)}) async-start(bf16[32,128,128]{2,1,0:T(8,128)(2,1)} %bitcast.9), calls=%async_computation.1 | async-start | bytes 2097152 | tf_op jit(solution)/shard_map/all_to_all | solution.py:181
  47.1 8.3 %collective-permute-done.5 = bf16[24,1,64,64]{3,2,1,0:T(8,128)(2,1)} collective-permute-done((bf16[24,1,64,64]{3,2,1,0:T(8,128)(2,1)}, bf16[24,1,64,64]{3,2,1,0:T(8,128)(2,1)}, u32[]{:S(2)}, u32[]{:S(2)}) %collective-permute-start.5) | collective-permute-done | bytes 196640 | tf_op jit(solution)/shard_map/ppermute | solution.py:28
  59.3 3.9 %collective-permute-done.7 = bf16[1,10,64,64]{3,2,1,0:T(8,128)(2,1)S(1)} collective-permute-done((bf16[1,10,64,64]{3,2,1,0:T(8,128)(2,1)S(1)}, bf16[1,10,64,64]{3,2,1,0:T(8,128)(2,1)S(1)}, u32[]{:S(2)}, u32[]{:S(2)}) %collective-permute-start.7) | collective-permute-done | bytes 81952 | tf_op jit(solution)/shard_map/ppermute | solution.py:28
  63.2 9.1 %select_maximum_fusion = bf16[26,10,66,64]{3,2,1,0:T(8,128)(2,1)S(1)} fusion(bf16[1,10,64,64]{3,2,1,0:T(8,128)(2,1)S(1)} %collective-permute-done.7, bf16[1,10,64,64]{3,2,1,0:T(8,128)(2,1)S(1)} %collective-permute-done.6, bf16[24,1,64,64]{3,2,1,0:T(8,128)(2,1)} %collective-permute-done.5, bf16[24,8,64,64]{3,2,1,0:T(8,128)(2,1)S(1)} %bitcast.161, ...), kind=kLoop, calls=%fused_computation.18 | loop fusion | flops 19768320 | bytes 4326400 | tf_op jit(solution)/shard_map/concatenate | solution.py:24
  74.7 20.4 %fusion.1 = f32[24,8,64,64]{3,2,1,0:T(8,128)} fusion(bf16[3,3,192,64]{3,2,1,0:T(8,128)(2,1)S(1)} %bitcast.188, bf16[26,10,64,64]{3,2,1,0:T(8,128)(2,1)S(1)} %get-tuple-element.32, bf16[1,10,64,64]{3,2,1,0:T(8,128)(2,1)S(1)} %collective-permute-done.7, bf16[24,1,64,64]{3,2,1,0:T(8,128)(2,1)} %collective-permute-done.5, ...), kind=kOutput, calls=%fused_computation.4 | convolution fusion | flops 2762637312 | bytes 9756672 | tf_op jit(solution)/shard_map/conv_general_dilated | solution.py:42
  95.0 16.0 %shard_map.78 = bf16[4096,128]{1,0:T(8,128)(2,1)} custom-call(s32[8192]{0:T(1024)S(1)} %compare_select_fusion.vox_ref, s32[32]{0:T(128)S(1)} %convert_reduce_fusion.1.count_ref, f32[12288,64]{1,0:T(8,128)} %bitcast.185), custom_call_target="tpu_custom_call" | custom-call | bytes 41943040 | tf_op jit(solution)/shard_map/pallas_call | solution.py:155
  111.0 17.9 %all-to-all-start.2 = ((bf16[32,128,128]{2,1,0:T(8,128)(2,1)}), bf16[32,128,128]{2,1,0:T(8,128)(2,1)S(1)}, u32[]{:S(2)}, u32[]{:S(2)}) async-start(bf16[32,128,128]{2,1,0:T(8,128)(2,1)} %bitcast.21), calls=%async_computation.2 | async-start | bytes 2097152 | tf_op jit(solution)/shard_map/all_to_all | solution.py:181
  129.0 20.8 %shard_map.77 = bf16[12288,64]{1,0:T(8,128)(2,1)} custom-call(s32[8192]{0:T(1024)S(1)} %bitcast.144, s32[32]{0:T(128)S(1)} %convert_reduce_fusion.1.count_ref, bf16[4096,128]{1,0:T(8,128)(2,1)S(1)} %bitcast.141), custom_call_target="tpu_custom_call" | custom-call | bytes 83886080 | tf_op jit(solution)/shard_map/pallas_call | solution.py:155
  151.1 3.1 collective-permute-start
  159.5 9.0 %collective-permute-done.1 = bf16[24,1,64,64]{3,2,1,0:T(8,128)(2,1)S(1)} collective-permute-done((bf16[24,1,64,64]{3,2,1,0:T(8,128)(2,1)S(1)}, bf16[24,1,64,64]{3,2,1,0:T(8,128)(2,1)S(1)}, u32[]{:S(2)}, u32[]{:S(2)}) %collective-permute-start.1) | collective-permute-done | bytes 196640 | tf_op jit(solution)/shard_map/ppermute | solution.py:28
  169.4 6.8 %collective-permute-start.2 = (bf16[1,10,64,64]{3,2,1,0:T(8,128)(2,1)}, bf16[1,10,64,64]{3,2,1,0:T(8,128)(2,1)}, u32[]{:S(2)}, u32[]{:S(2)}) collective-permute-start(bf16[1,10,64,64]{3,2,1,0:T(8,128)(2,1)} %get-tuple-element.37), channel_id=1, source_target_pairs={{0,1},{1,2},{2,3},{3,4},{4,5},{5,6},{6,7},{8,9},{9,10},{10,11},{11... | collective-permute-start | bytes 245768 | tf_op jit(solution)/shard_map/ppermute | solution.py:26
  177.5 6.8 %shard_map.79 = f32[4096,64]{1,0:T(8,128)S(1)} custom-call(s32[4096]{0:T(1024)S(1)} %fusion.40.place_ref, bf16[4096,128]{1,0:T(8,128)(2,1)S(1)} %bitcast.142), custom_call_target="tpu_custom_call" | custom-call | bytes 41943040 | tf_op jit(solution)/shard_map/pallas_call | solution.py:155
  188.0 9.1 %select_maximum_fusion.4 = bf16[26,10,66,64]{3,2,1,0:T(8,128)(2,1)S(1)} fusion(bf16[1,10,64,64]{3,2,1,0:T(8,128)(2,1)} %collective-permute-done.3, bf16[1,10,64,64]{3,2,1,0:T(8,128)(2,1)} %collective-permute-done.2, bf16[24,1,64,64]{3,2,1,0:T(8,128)(2,1)} %copy-done.9, bf16[24,8,64,64]{3,2,1,0:T(8,128)(2,1)S(1)} %bitcast.157, ...), kind=kLoop, calls=%fused_computation.22 | loop fusion | flops 19768320 | bytes 4326400 | tf_op jit(solution)/shard_map/concatenate | solution.py:24
  199.4 10.3 %pad_maximum_fusion = bf16[26,10,64,192]{3,2,1,0:T(8,128)(2,1)} fusion(bf16[26,10,64,64]{3,2,1,0:T(8,128)(2,1)S(1)} %get-tuple-element.34, bf16[1,10,64,64]{3,2,1,0:T(8,128)(2,1)} %collective-permute-done.3, bf16[24,1,64,64]{3,2,1,0:T(8,128)(2,1)S(1)} %copy-done.10, bf16[24,8,64,64]{3,2,1,0:T(8,128)(2,1)S(1)} %bitcast.158, ...), kind=kLoop, calls=%fused_computation.3 | loop fusion | flops 44728320 | bytes 12779520 | tf_op jit(solution)/shard_map/concatenate | solution.py:38
  209.7 37.2 %fusion.48 = (bf16[24,8,64,192]{3,2,1,0:T(8,128)(2,1)}, bf16[24,8,64,192]{3,2,1,0:T(8,128)(2,1)}, bf16[24,8,64,192]{3,2,1,0:T(8,128)(2,1)}, bf16[24,8,64,192]{3,...) fusion(bf16[26,10,64,192]{3,2,1,0:T(8,128)(2,1)} %pad_maximum_f, ...), kind=kLoop, calls=%fused_computation.92 | loop fusion | bytes 84934656 | tf_op jit(solution)/shard_map/slice | solution.py:255
  246.9 4.1 %fusion.31 = f32[9,64,192]{2,1,0:T(8,128)S(1)} fusion(bf16[64,12288]{1,0:T(8,128)(2,1)S(1)} %bitcast.146, bf16[12288,192]{1,0:T(8,128)(2,1)} %bitcast.183), kind=kOutput, calls=%fused_computation.51 | convolution fusion | flops 301989888 | bytes 6356992 | tf_op jit(solution)/shard_map/ov,vk->ok/dot_general | solution.py:256
  268.0 11.1 %all-to-all-start.3 = ((f32[32,1,3456]{2,1,0:T(1,128)}), f32[32,1,3456]{2,1,0:T(1,128)}, u32[]{:S(2)}, u32[]{:S(2)}) async-start(f32[32,1,3456]{2,1,0:T(1,128)} %all_to_all.21), calls=%async_computation.3 | async-start | bytes 884736 | tf_op jit(solution)/shard_map/all_to_all | solution.py:181
  279.2 17.1 %convolution_convert_fusion = bf16[64,24,8,64]{0,3,2,1:T(8,128)(2,1)S(1)} fusion(bf16[26,10,64,192]{3,2,1,0:T(8,128)(2,1)} %pad_maximum_fusion, bf16[3,3,64,192]{3,2,1,0:T(8,128)(2,1)S(1)} %bitcast.189), kind=kOutput, calls=%fused_computation.29 | convolution fusion | flops 2718695424 | bytes 8183808 | tf_op jit(solution)/shard_map/conv_general_dilated | solution.py:42
  296.2 3.1 copy.44
  300.7 43.2 %all-gather = f32[32,1,3456]{2,1,0:T(1,128)S(1)} all-gather(f32[1,1,3456]{2,1,0:T(1,128)S(1)} %reshape.164), channel_id=1, replica_groups=mesh['narrow'=4,'region'=8] {'narrow','region'}, dimensions={0}, use_global_device_ids=true | all-gather | bytes 456192 | tf_op jit(solution)/shard_map/all_gather | solution.py:260
  (112 shorter events, 54.8 us)
Async XLA Ops:
  0.6 35.0 %copy-start.12 = (bf16[9,64,192]{2,1,0:T(8,128)(2,1)S(1)}, bf16[9,64,192]{2,1,0:T(8,128)(2,1)}, u32[]{:S(2)}) copy-start(bf16[9,64,192]{2,1,0:T(8,128)(2,1)} %param.8) | copy-start | bytes 663556
  18.2 22.2 %all-to-all-start = ((s32[32,1,256]{2,1,0:T(1,128)}), s32[32,1,256]{2,1,0:T(1,128)S(1)}, u32[]{:S(2)}, u32[]{:S(2)}) async-start(s32[32,1,256]{2,1,0:T(1,128)} %copy.38), calls=%async_computation | async-start | bytes 65536 | tf_op jit(solution)/shard_map/all_to_all | solution.py:181
  28.9 11.5 %copy-start.4 = (bf16[64,24,512]{0,2,1:T(8,128)(2,1)}, bf16[64,24,512]{0,2,1:T(8,128)(2,1)S(1)}, u32[]{:S(2)}) copy-start(bf16[64,24,512]{0,2,1:T(8,128)(2,1)S(1)} %copy.40) | copy-start | bytes 4718596
  29.9 17.2 %collective-permute-start.4 = (bf16[24,1,64,64]{3,2,1,0:T(8,128)(2,1)}, bf16[24,1,64,64]{3,2,1,0:T(8,128)(2,1)}, u32[]{:S(2)}, u32[]{:S(2)}) collective-permute-start(bf16[24,1,64,64]{3,2,1,0:T(8,128)(2,1)} %get-tuple-element.39), channel_id=1, source_target_pairs={{0,8},{8,16},{16,24},{1,9},{9,17},{17,25},{2,10},{10,18},{18,26},{... | collective-permute-start | bytes 589832 | tf_op jit(solution)/shard_map/ppermute | solution.py:26
  34.3 21.2 %collective-permute-start.5 = (bf16[24,1,64,64]{3,2,1,0:T(8,128)(2,1)}, bf16[24,1,64,64]{3,2,1,0:T(8,128)(2,1)}, u32[]{:S(2)}, u32[]{:S(2)}) collective-permute-start(bf16[24,1,64,64]{3,2,1,0:T(8,128)(2,1)} %get-tuple-element.40), channel_id=1, source_target_pairs={{8,0},{16,8},{24,16},{9,1},{17,9},{25,17},{10,2},{18,10},{26,18},{... | collective-permute-start | bytes 589832 | tf_op jit(solution)/shard_map/ppermute | solution.py:28
  40.4 70.7 %all-to-all-start.1 = ((bf16[32,128,128]{2,1,0:T(8,128)(2,1)}), bf16[32,128,128]{2,1,0:T(8,128)(2,1)S(1)}, u32[]{:S(2)}, u32[]{:S(2)}) async-start(bf16[32,128,128]{2,1,0:T(8,128)(2,1)} %bitcast.9), calls=%async_computation.1 | async-start | bytes 2097152 | tf_op jit(solution)/shard_map/all_to_all | solution.py:181
  47.1 16.1 %copy-start.5 = (bf16[64,24,512]{0,2,1:T(8,128)(2,1)S(1)}, bf16[64,24,512]{0,2,1:T(8,128)(2,1)}, u32[]{:S(2)}) copy-start(bf16[64,24,512]{0,2,1:T(8,128)(2,1)} %copy-done.4) | copy-start | bytes 4718596
  56.6 2.7 collective-permute-start.6
  57.9 5.3 %collective-permute-start.7 = (bf16[1,10,64,64]{3,2,1,0:T(8,128)(2,1)S(1)}, bf16[1,10,64,64]{3,2,1,0:T(8,128)(2,1)S(1)}, u32[]{:S(2)}, u32[]{:S(2)}) collective-permute-start(bf16[1,10,64,64]{3,2,1,0:T(8,128)(2,1)S(1)} %get-tuple-element.36), channel_id=1, source_target_pairs={{1,0},{2,1},{3,2},{4,3},{5,4},{6,5},{7,6},{9,8},{10,9},{11,10},{12... | collective-permute-start | bytes 245768 | tf_op jit(solution)/shard_map/ppermute | solution.py:28
  111.0 66.5 %all-to-all-start.2 = ((bf16[32,128,128]{2,1,0:T(8,128)(2,1)}), bf16[32,128,128]{2,1,0:T(8,128)(2,1)S(1)}, u32[]{:S(2)}, u32[]{:S(2)}) async-start(bf16[32,128,128]{2,1,0:T(8,128)(2,1)} %bitcast.21), calls=%async_computation.2 | async-start | bytes 2097152 | tf_op jit(solution)/shard_map/all_to_all | solution.py:181
  129.0 26.7 %copy-start.8 = (bf16[64,24,512]{2,1,0:T(8,128)(2,1)S(1)}, bf16[64,24,512]{2,1,0:T(8,128)(2,1)}, u32[]{:S(2)}) copy-start(bf16[64,24,512]{2,1,0:T(8,128)(2,1)} %param.9) | copy-start | bytes 4718596
  149.8 18.7 %copy-start.2 = (bf16[12288,64]{1,0:T(8,128)(2,1)S(1)}, bf16[12288,64]{1,0:T(8,128)(2,1)}, u32[]{:S(2)}) copy-start(bf16[12288,64]{1,0:T(8,128)(2,1)} %shard_map.77) | copy-start | bytes 4718596
  151.1 8.4 %collective-permute-start = (bf16[24,1,64,64]{3,2,1,0:T(8,128)(2,1)S(1)}, bf16[24,1,64,64]{3,2,1,0:T(8,128)(2,1)S(1)}, u32[]{:S(2)}, u32[]{:S(2)}) collective-permute-start(bf16[24,1,64,64]{3,2,1,0:T(8,128)(2,1)S(1)} %get-tuple-element.41), channel_id=1, source_target_pairs={{0,8},{8,16},{16,24},{1,9},{9,17},{17,25},{2,10},{10,18},{18,26},{... | collective-permute-start | bytes 589832 | tf_op jit(solution)/shard_map/ppermute | solution.py:26
  154.2 14.3 %collective-permute-start.1 = (bf16[24,1,64,64]{3,2,1,0:T(8,128)(2,1)S(1)}, bf16[24,1,64,64]{3,2,1,0:T(8,128)(2,1)S(1)}, u32[]{:S(2)}, u32[]{:S(2)}) collective-permute-start(bf16[24,1,64,64]{3,2,1,0:T(8,128)(2,1)S(1)} %get-tuple-element.42), channel_id=1, source_target_pairs={{8,0},{16,8},{24,16},{9,1},{17,9},{25,17},{10,2},{18,10},{26,18},{... | collective-permute-start | bytes 589832 | tf_op jit(solution)/shard_map/ppermute | solution.py:28
  168.5 9.0 %copy-start.9 = (bf16[24,1,64,64]{3,2,1,0:T(8,128)(2,1)}, bf16[24,1,64,64]{3,2,1,0:T(8,128)(2,1)S(1)}, u32[]{:S(2)}) copy-start(bf16[24,1,64,64]{3,2,1,0:T(8,128)(2,1)S(1)} %collective-permute-done.1) | copy-start | bytes 589828
  169.4 18.6 %collective-permute-start.2 = (bf16[1,10,64,64]{3,2,1,0:T(8,128)(2,1)}, bf16[1,10,64,64]{3,2,1,0:T(8,128)(2,1)}, u32[]{:S(2)}, u32[]{:S(2)}) collective-permute-start(bf16[1,10,64,64]{3,2,1,0:T(8,128)(2,1)} %get-tuple-element.37), channel_id=1, source_target_pairs={{0,1},{1,2},{2,3},{3,4},{4,5},{5,6},{6,7},{8,9},{9,10},{10,11},{11... | collective-permute-start | bytes 245768 | tf_op jit(solution)/shard_map/ppermute | solution.py:26
  176.2 11.7 %collective-permute-start.3 = (bf16[1,10,64,64]{3,2,1,0:T(8,128)(2,1)}, bf16[1,10,64,64]{3,2,1,0:T(8,128)(2,1)}, u32[]{:S(2)}, u32[]{:S(2)}) collective-permute-start(bf16[1,10,64,64]{3,2,1,0:T(8,128)(2,1)} %get-tuple-element.38), channel_id=1, source_target_pairs={{1,0},{2,1},{3,2},{4,3},{5,4},{6,5},{7,6},{9,8},{10,9},{11,10},{12... | collective-permute-start | bytes 245768 | tf_op jit(solution)/shard_map/ppermute | solution.py:28
  209.7 37.2 %copy-start.1 = (bf16[8,8,24,512]{3,1,2,0:T(8,128)(2,1)S(1)}, bf16[8,8,24,512]{3,1,2,0:T(8,128)(2,1)}, u32[]{:S(2)}) copy-start(bf16[8,8,24,512]{3,1,2,0:T(8,128)(2,1)} %copy.46) | copy-start | bytes 4718596
  246.9 4.6 %copy-start.7 = (bf16[24,8,64,192]{3,2,1,0:T(8,128)(2,1)S(1)}, bf16[24,8,64,192]{3,2,1,0:T(8,128)(2,1)}, u32[]{:S(2)}) copy-start(bf16[24,8,64,192]{3,2,1,0:T(8,128)(2,1)} %get-tuple-element.29) | copy-start | bytes 14155780
  246.9 6.4 %copy-start.6 = (bf16[24,8,64,192]{3,2,1,0:T(8,128)(2,1)S(1)}, bf16[24,8,64,192]{3,2,1,0:T(8,128)(2,1)}, u32[]{:S(2)}) copy-start(bf16[24,8,64,192]{3,2,1,0:T(8,128)(2,1)} %get-tuple-element.28) | copy-start | bytes 14155780
  251.5 6.2 %slice-start.8 = ((s8[6291456]{0:T(1024)(128)(4,1)}), s8[4194304]{0:T(1024)(128)(4,1)S(1)}, s32[]{:S(2)}) async-start(s8[6291456]{0:T(1024)(128)(4,1)} %bitcast.175), calls=%async_computation.12 | async-start | bytes 8388608
  256.5 5.4 %slice-start.4 = ((s8[6291456]{0:T(1024)(128)(4,1)}), s8[4194304]{0:T(1024)(128)(4,1)S(1)}, s32[]{:S(2)}) async-start(s8[6291456]{0:T(1024)(128)(4,1)} %bitcast.169), calls=%async_computation.8 | async-start | bytes 8388608
  264.8 14.3 %copy-start.13 = (bf16[9,64,192]{2,1,0:T(8,128)(2,1)S(1)}, bf16[9,64,192]{2,1,0:T(8,128)(2,1)}, u32[]{:S(2)}) copy-start(bf16[9,64,192]{2,1,0:T(8,128)(2,1)} %param.8) | copy-start | bytes 663556
  268.0 31.4 %all-to-all-start.3 = ((f32[32,1,3456]{2,1,0:T(1,128)}), f32[32,1,3456]{2,1,0:T(1,128)}, u32[]{:S(2)}, u32[]{:S(2)}) async-start(f32[32,1,3456]{2,1,0:T(1,128)} %all_to_all.21), calls=%async_computation.3 | async-start | bytes 884736 | tf_op jit(solution)/shard_map/all_to_all | solution.py:181
  (14 other events, 41.5 us)

commit v2 on v1

--- a/solution.py
+++ b/solution.py
@@ -15,27 +15,113 @@
 TILE = 512
 
 
-def extended(cells, sides):
-    for axis, dim in sides:
-        count = lax.axis_size(axis)
-        ends = count - 1
-        head = lax.slice_in_dim(cells, 0, 1, axis=dim)
-        tail = lax.slice_in_dim(cells, cells.shape[dim] - 1, cells.shape[dim], axis=dim)
-        cells = jnp.concatenate(
-            [
-                lax.ppermute(tail, axis, [(i, (i + 1) % count) for i in range(ends)]),
-                cells,
-                lax.ppermute(head, axis, [((i + 1) % count, i) for i in range(ends)]),
-            ],
-            axis=dim,
+def halo_kernel(n_narrow, n_region, grid, left, right, top, bottom, send, recv):
+    n, r = lax.axis_index("narrow"), lax.axis_index("region")
+    west, east = lax.rem(n + n_narrow - 1, n_narrow), lax.rem(n + 1, n_narrow)
+    north, south = lax.rem(r + n_region - 1, n_region), lax.rem(r + 1, n_region)
+    last = grid.shape[0] - 1
+    moves = [
+        ((west, r), grid.at[:, 0], right),
+        ((east, r), grid.at[:, CY - 1], left),
+        ((n, north), grid.at[0], bottom.at[pl.ds(1, CY)]),
+        ((n, south), grid.at[last], top.at[pl.ds(1, CY)]),
+        ((west, north), grid.at[0, 0], bottom.at[CY + 1]),
+        ((east, north), grid.at[0, CY - 1], bottom.at[0]),
+        ((west, south), grid.at[last, 0], top.at[CY + 1]),
+        ((east, south), grid.at[last, CY - 1], top.at[0]),
+    ]
+    barrier = pltpu.get_barrier_semaphore()
+    for device, _, _ in moves:
+        pl.semaphore_signal(barrier, inc=1, device_id=device, device_id_type=pl.DeviceIdType.MESH)
+    pl.semaphore_wait(barrier, len(moves))
+    copies = [
+        pltpu.make_async_remote_copy(
+            src_ref=source,
+            dst_ref=target,
+            send_sem=send.at[i],
+            recv_sem=recv.at[i],
+            device_id=device,
+            device_id_type=pl.DeviceIdType.MESH,
         )
-    return cells
-
-
-def stacked_depth(cells):
-    padded = extended(cells, (("narrow", 1), ("region", 0)))
-    padded = jnp.pad(padded, ((0, 0), (0, 0), (1, 1), (0, 0)))
-    return jnp.concatenate([padded[:, :, d : d + NZ] for d in range(3)], axis=3)
+        for i, (device, source, target) in enumerate(moves)
+    ]
+    for copy in copies:
+        copy.start()
+    for copy in copies:
+        copy.wait()
+
+
+def halos(grid, n_narrow, n_region, collective_id):
+    rows_x, _, depth, chans = grid.shape
+    side = jax.ShapeDtypeStruct((rows_x, depth, chans), grid.dtype)
+    end = jax.ShapeDtypeStruct((CY + 2, depth, chans), grid.dtype)
+    anywhere = pl.BlockSpec(memory_space=pl.ANY)
+    return pl.pallas_call(
+        functools.partial(halo_kernel, n_narrow, n_region),
+        out_shape=(side, side, end, end),
+        in_specs=[anywhere],
+        out_specs=[anywhere] * 4,
+        scratch_shapes=[pltpu.SemaphoreType.DMA((8,)), pltpu.SemaphoreType.DMA((8,))],
+        compiler_params=pltpu.CompilerParams(collective_id=collective_id, has_side_effects=True),
+        cost_estimate=pl.CostEstimate(flops=0, bytes_accessed=10 << 20, transcendentals=0),
+    )(grid)
+
+
+def stack_kernel(inside_ref, center, left, right, top, bottom, out):
+    rows_x, _, depth, chans = center.shape
+    f32 = jnp.float32
+    row = lax.broadcasted_iota(jnp.int32, (depth, chans), 0)
+    west, east, north, south = [inside_ref[i] for i in range(4)]
+
+    def spread(tile, keep=None):
+        t = tile.astype(f32)
+        if keep is not None:
+            t = jnp.where(keep > 0, t, 0.0)
+        up = jnp.where(row == 0, 0.0, pltpu.roll(t, 1, 0))
+        down = jnp.where(row == depth - 1, 0.0, pltpu.roll(t, depth - 1, 0))
+        return jnp.concatenate([up, t, down], axis=1).astype(jnp.bfloat16)
+
+    def plane(x, _):
+        out[x + 1, 0] = spread(left[x], west)
+        out[x + 1, CY + 1] = spread(right[x], east)
+        for y in range(CY):
+            out[x + 1, y + 1] = spread(center[x, y])
+
+    lax.fori_loop(0, rows_x, plane, None)
+    for at, end, keep in ((0, top, north), (rows_x + 1, bottom, south)):
+        out[at, 0] = spread(end[0], keep * west)
+        out[at, CY + 1] = spread(end[CY + 1], keep * east)
+        for y in range(1, CY + 1):
+            out[at, y] = spread(end[y], keep)
+
+
+def stack_weight_kernel(inside_ref, center, left, right, top, bottom, flat, out, sums):
+    stack_kernel(inside_ref, center, left, right, top, bottom, out)
+    sums[...] = jnp.zeros_like(sums)
+    plane_cells = CY * NZ
+
+    def plane(x, _):
+        here = flat[:, pl.ds(pl.multiple_of(x * plane_cells, plane_cells), plane_cells)]
+        for a in range(3):
+            for b in range(3):
+                window = out[x + a, b : b + CY].reshape(plane_cells, out.shape[3])
+                sums[3 * a + b] += jnp.dot(here, window, preferred_element_type=jnp.float32)
+
+    lax.fori_loop(0, center.shape[0], plane, None)
+
+
+def stacked_depth(cells, n_narrow, n_region, collective_id, flat=None):
+    rows_x, _, depth, chans = cells.shape
+    n, r = lax.axis_index("narrow"), lax.axis_index("region")
+    inside = jnp.stack([n > 0, n < n_narrow - 1, r > 0, r < n_region - 1]).astype(jnp.int32)
+    edges = halos(cells, n_narrow, n_region, collective_id)
+    stack = jax.ShapeDtypeStruct((rows_x + 2, CY + 2, depth, 3 * chans), cells.dtype)
+    if flat is None:
+        return call(stack_kernel, stack, "svvvvv", "v", [], 40 << 20, inside, cells, *edges)
+    sums = jax.ShapeDtypeStruct((9, chans, 3 * chans), jnp.float32)
+    return call(
+        stack_weight_kernel, (stack, sums), "svvvvvv", "vv", [], 80 << 20, inside, cells, *edges, flat
+    )
 
 
 def convolved(stack, kernel):
@@ -222,7 +308,7 @@
     forward = weight.reshape(3, 3, chans, 3 * chans).transpose(0, 1, 3, 2)
 
     grads = cotangent.reshape(chans, rows_x, CY, NZ).transpose(1, 2, 3, 0)
-    table = convolved(stacked_depth(grads), backward).reshape(voxels, chans)
+    table = convolved(stacked_depth(grads, n_narrow, n_region, 0), backward).reshape(voxels, chans)
     picked = call(
         functools.partial(pick_kernel, devices, slots),
         pairs,
@@ -247,17 +333,14 @@
         count,
         got,
     )
-    stack = stacked_depth(grid.reshape(rows_x, CY, NZ, chans))
-    flat = cotangent.reshape(chans, voxels)
-    kernels = []
-    for a in range(3):
-        for b in range(3):
-            window = stack[a : a + rows_x, b : b + CY].reshape(voxels, 3 * chans)
-            kernels.append(jnp.einsum("ov,vk->ok", flat, window, preferred_element_type=f32))
+    cells = grid.reshape(rows_x, CY, NZ, chans)
+    stack, kernels = stacked_depth(cells, n_narrow, n_region, 1, cotangent.reshape(chans, voxels))
     total_cells = rows_x * n_region * CY * n_narrow * NZ
-    parts = exchanged(jnp.stack(kernels).reshape(devices, -1))
+    parts = exchanged(kernels.reshape(devices, -1))
     mine = jnp.sum(parts, axis=0) * (1.0 / math.sqrt(total_cells))
-    weight_grad = lax.all_gather(mine, AXES, tiled=True).reshape(9, chans, 3 * chans)
+    back, mine = lax.optimization_barrier((back, mine))
+    everywhere = exchanged(jnp.broadcast_to(mine, (devices, mine.shape[0])))
+    weight_grad = everywhere.reshape(9, chans, 3 * chans)
 
     result = convolved(stack, forward).astype(bf16)
     conv_out = result.transpose(3, 0, 1, 2).reshape(chans, rows_x, CY * NZ)

time: 342 us -> 258 us (0.75); the launches traced: 346 us -> 257 us
  Pallas kernels: 54.3 us -> 142 us
  starting transfers between devices: 64 us -> 14.6 us
  local copies, waits for them, and re-layouts: 71.1 us -> 26.2 us
  other arithmetic: 36.6 us -> 5.3 us
  blocking collectives: 43.2 us -> 14.3 us
  matrix products: 52.1 us -> 35.4 us
  waiting for transfers between devices: 23.4 us -> 17.8 us
    pallas_call x0 -> x2, Pallas kernels: none -> 52.1 us  [halos(): pl.pallas_call(functools.partial(halo_kernel, n_narrow, n_region), out_sh...]
    slice x5 -> x0, local copies, waits for them, and re-layouts: 44.2 us -> none  [the longest x1 37.2 us: shards(): window = stack[a:a + rows_x, b:b + CY].reshape(voxels, 3 * chans)]
    all_gather x1 -> x0, blocking collectives: 43.2 us -> none  [shards(): lax.all_gather(mine, AXES, tiled=True).reshape(9, chans, 3 * chans)]
    pallas_call x4 -> x6, Pallas kernels: 54.3 us -> 90.2 us  [call(): pl.pallas_call(kernel, out_shape=out_shape, in_specs=[pl.BlockSpec(memory...]
    all_to_all x4, starting transfers between devices: 43.1 us -> 14.6 us  [exchanged(): return lax.all_to_all(x, AXES, split_axis=0, concat_axis=0, tiled=True)]
    concatenate x3 -> x0, other arithmetic: 28.4 us -> none  [the longest x2 18.1 us: extended(): jnp.concatenate([lax.ppermute(tail, axis, [(i, (i + 1) % count) for i in...]
    ppermute x8 -> x0, waiting for transfers between devices: 23.4 us -> none  [the longest x4 21.3 us: extended(): lax.ppermute(head, axis, [((i + 1) % count, i) for i in range(ends)])]
    ppermute x8 -> x0, starting transfers between devices: 21 us -> none  [the longest x4 15.6 us: extended(): lax.ppermute(tail, axis, [(i, (i + 1) % count) for i in range(ends)])]
  transfers between devices with their start and end apart: 12 -> 4, of which waited for: 4 -> 2; matrix products, arithmetic and copies ran while one was open for 20% -> 19% of each run, Pallas kernels for 13% -> 22%
where the time goes in v2:
time: 258 us; the launch traced here: 257 us
  Pallas kernels  142 us (55%)
  matrix products  35.4 us (14%)
  local copies, waits for them, and re-layouts  26.2 us (10%)
  waiting for transfers between devices  17.8 us (7%)
  starting transfers between devices  14.6 us (6%)
  blocking collectives  14.3 us (6%)
  other arithmetic  5.3 us (2%)
    pallas_call x6, Pallas kernels, call(): pl.pallas_call(kernel, out_shape=out_shape, in_specs=[pl.BlockSpec(memory...  90.2 us
    pallas_call x2, Pallas kernels, halos(): pl.pallas_call(functools.partial(halo_kernel, n_narrow, n_region), out_sh...  52.1 us
    conv_general_dilated x2, matrix products, convolved(): lax.conv_general_dilated(stack, kernel, (1, 1), 'VALID', dimension_number...  34.2 us
    unnamed x27, local copies, waits for them, and re-layouts  21.1 us
    all_to_all x4, waiting for transfers between devices, exchanged(): return lax.all_to_all(x, AXES, split_axis=0, concat_axis=0, tiled=True)  17.8 us
    all_to_all x4, starting transfers between devices, exchanged(): return lax.all_to_all(x, AXES, split_axis=0, concat_axis=0, tiled=True)  14.6 us
    all_to_all x1, blocking collectives, exchanged(): return lax.all_to_all(x, AXES, split_axis=0, concat_axis=0, tiled=True)  14.3 us
  transfers between devices with their start and end apart: 4, of which 2 were waited for; matrix products, arithmetic and copies ran while one was open for 19% of the time, Pallas kernels for 22%

profile of v2, /device:TPU:0, one launch (start us, length us, event | category | flops | bytes accessed | tf_op | source)
XLA Modules:
  0.0 256.7 jit_solution(12346528949174914800)
XLA Ops:
  4.4 1.4 copy.36
  6.6 10.7 %shard_map.76 = (bf16[4096,128]{1,0:T(8,128)(2,1)}, s32[8192]{0:T(1024)S(1)}) custom-call(s32[4096]{0:T(1024)S(1)} %fusion.11.place_ref, s32[4096]{0:T(1024)S(1)} %copy-done.8, f32[4096,64]{1,0:T(8,128)S(1)} %bitcast.64), custom_call_target="tpu_custom_call" | custom-call | bytes 41943040 | tf_op jit(solution)/shard_map/pallas_call | solution.py:241
  17.5 14.3 %all_to_all.32 = s32[32,1,256]{2,1,0:T(1,128)S(1)} all-to-all(s32[32,1,256]{2,1,0:T(1,128)S(1)} %copy.38), channel_id=1, replica_groups=mesh['narrow'=4,'region'=8] {'narrow','region'}, dimensions={0} | all-to-all | bytes 65536 | tf_op jit(solution)/shard_map/all_to_all | solution.py:267
  31.8 2.8 %all-to-all-start.1 = ((bf16[32,128,128]{2,1,0:T(8,128)(2,1)}), bf16[32,128,128]{2,1,0:T(8,128)(2,1)S(1)}, u32[]{:S(2)}, u32[]{:S(2)}) async-start(bf16[32,128,128]{2,1,0:T(8,128)(2,1)} %bitcast.13), calls=%async_computation.1 | async-start | bytes 2097152 | tf_op jit(solution)/shard_map/all_to_all | solution.py:267
  34.6 4.6 %copy.40 = bf16[64,24,512]{0,2,1:T(8,128)(2,1)} copy(bf16[64,24,512]{2,1,0:T(8,128)(2,1)} %param.9) | data formatting | bytes 3145728 | tf_op args[4]
  39.2 2.0 copy.46
  41.2 28.9 %shard_map.80 = (bf16[24,64,64]{2,1,0:T(8,128)(2,1)}, bf16[24,64,64]{2,1,0:T(8,128)(2,1)}, bf16[10,64,64]{2,1,0:T(8,128)(2,1)}, bf16[10,64,64]{2,1,0:T(8,128)(2,1)}) custom-call(bf16[24,8,64,64]{3,2,1,0:T(8,128)(2,1)} %bitcast.73), custom_call_target="tpu_custom_call" | custom-call | bytes 10485760 | tf_op jit(solution)/shard_map/pallas_call | solution.py:59
  74.6 8.5 %shard_map.81 = bf16[26,10,64,192]{3,2,1,0:T(8,128)(2,1)} custom-call(s32[4]{0:T(128)S(1)} %add_convert_fusion.inside_ref, bf16[24,8,64,64]{3,2,1,0:T(8,128)(2,1)} %bitcast.74, bf16[24,64,64]{2,1,0:T(8,128)(2,1)S(1)} %copy-done, bf16[24,64,64]{2,1,0:T(8,128)(2,1)S(1)} %copy-done.1, bf16[10,64,64]{2,1,0:T(8,128)(2,1)S(1)} %copy-done.6, ...), custom_call_target="tpu_custom_call" | custom-call | bytes 41943040 | tf_op jit(solution)/shard_map/pallas_call | solution.py:241
  83.2 24.2 %shard_map.77 = bf16[12288,64]{1,0:T(8,128)(2,1)} custom-call(s32[8192]{0:T(1024)S(1)} %bitcast.68, s32[32]{0:T(128)S(1)} %convert_reduce_fusion.1.count_ref, bf16[4096,128]{1,0:T(8,128)(2,1)S(1)} %bitcast.66), custom_call_target="tpu_custom_call" | custom-call | bytes 83886080 | tf_op jit(solution)/shard_map/pallas_call | solution.py:241
  107.4 23.2 %shard_map.78 = (bf16[24,64,64]{2,1,0:T(8,128)(2,1)}, bf16[24,64,64]{2,1,0:T(8,128)(2,1)}, bf16[10,64,64]{2,1,0:T(8,128)(2,1)}, bf16[10,64,64]{2,1,0:T(8,128)(2,1)}) custom-call(bf16[24,8,64,64]{3,2,1,0:T(8,128)(2,1)} %bitcast.71), custom_call_target="tpu_custom_call" | custom-call | bytes 10485760 | tf_op jit(solution)/shard_map/pallas_call | solution.py:59
  134.4 20.9 %shard_map.79 = (bf16[26,10,64,192]{3,2,1,0:T(8,128)(2,1)}, f32[9,64,192]{2,1,0:T(8,128)S(1)}) custom-call(s32[4]{0:T(128)S(1)} %add_convert_fusion.inside_ref, bf16[24,8,64,64]{3,2,1,0:T(8,128)(2,1)} %bitcast.72, bf16[24,64,64]{2,1,0:T(8,128)(2,1)S(1)} %copy-done.2, bf16[24,64,64]{2,1,0:T(8,128)(2,1)S(1)} %copy-done.3, bf16[10,64,64]{2,1,0:T(8,128)(2,1)S(1)} %copy-done.4, ...), custom_call_target="tpu_custom_call" | custom-call | bytes 83886080 | tf_op jit(solution)/shard_map/pallas_call | solution.py:241
  155.3 1.3 all_to_all.26
  156.7 3.0 %all-to-all-start.3 = ((f32[32,1,3456]{2,1,0:T(1,128)}), f32[32,1,3456]{2,1,0:T(1,128)S(1)}, u32[]{:S(2)}, u32[]{:S(2)}) async-start(f32[32,1,3456]{2,1,0:T(1,128)} %all_to_all.26), calls=%async_computation.3 | async-start | bytes 884736 | tf_op jit(solution)/shard_map/all_to_all | solution.py:267
  159.7 16.2 %fusion.18 = f32[24,8,64,64]{3,2,1,0:T(8,128)} fusion(bf16[26,10,64,192]{3,2,1,0:T(8,128)(2,1)} %shard_map.81, bf16[3,3,192,64]{3,2,1,0:T(8,128)(2,1)S(1)} %bitcast.79), kind=kOutput, calls=%fused_computation.39 | convolution fusion | flops 2717908992 | bytes 9756672 | tf_op jit(solution)/shard_map/conv_general_dilated | solution.py:128
  175.8 19.1 %shard_map.82 = bf16[4096,128]{1,0:T(8,128)(2,1)} custom-call(s32[8192]{0:T(1024)S(1)} %compare_select_fusion.vox_ref, s32[32]{0:T(128)S(1)} %convert_reduce_fusion.1.count_ref, f32[12288,64]{1,0:T(8,128)} %bitcast.76), custom_call_target="tpu_custom_call" | custom-call | bytes 41943040 | tf_op jit(solution)/shard_map/pallas_call | solution.py:241
  194.9 5.5 %all-to-all-start.2 = ((bf16[32,128,128]{2,1,0:T(8,128)(2,1)}), bf16[32,128,128]{2,1,0:T(8,128)(2,1)S(1)}, u32[]{:S(2)}, u32[]{:S(2)}) async-start(bf16[32,128,128]{2,1,0:T(8,128)(2,1)} %bitcast.25), calls=%async_computation.2 | async-start | bytes 2097152 | tf_op jit(solution)/shard_map/all_to_all | solution.py:267
  200.4 18.1 %convolution_convert_fusion = bf16[64,24,8,64]{0,3,2,1:T(8,128)(2,1)} fusion(bf16[26,10,64,192]{3,2,1,0:T(8,128)(2,1)} %get-tuple-element.23, bf16[3,3,64,192]{3,2,1,0:T(8,128)(2,1)S(1)} %bitcast.80), kind=kOutput, calls=%fused_computation | convolution fusion | flops 2718695424 | bytes 8183808 | tf_op jit(solution)/shard_map/conv_general_dilated | solution.py:128
  218.5 4.8 %copy.44 = bf16[64,24,512]{2,1,0:T(8,128)(2,1)} copy(bf16[64,24,512]{0,2,1:T(8,128)(2,1)} %bitcast.77) | data formatting | bytes 3145728
  223.6 4.4 %all-to-all-done.2 = bf16[32,128,128]{2,1,0:T(8,128)(2,1)S(1)} async-done(((bf16[32,128,128]{2,1,0:T(8,128)(2,1)}), bf16[32,128,128]{2,1,0:T(8,128)(2,1)S(1)}, u32[]{:S(2)}, u32[]{:S(2)}) %all-to-all-start.2) | async-done | bytes 1048608 | tf_op jit(solution)/shard_map/all_to_all | solution.py:267
  228.0 6.8 %shard_map.83 = f32[4096,64]{1,0:T(8,128)S(1)} custom-call(s32[4096]{0:T(1024)S(1)} %fusion.11.place_ref, bf16[4096,128]{1,0:T(8,128)(2,1)S(1)} %bitcast.67), custom_call_target="tpu_custom_call" | custom-call | bytes 41943040 | tf_op jit(solution)/shard_map/pallas_call | solution.py:241
  235.8 3.3 %all-to-all-start.4 = ((f32[32,1,3456]{2,1,0:T(1,128)}), f32[32,1,3456]{2,1,0:T(1,128)}, u32[]{:S(2)}, u32[]{:S(2)}) async-start(f32[32,1,3456]{2,1,0:T(1,128)} %broadcast_in_dim.28), calls=%async_computation.4 | async-start | bytes 884736 | tf_op jit(solution)/shard_map/all_to_all | solution.py:267
  239.2 1.1 copy.45
  240.3 13.3 %all-to-all-done.4 = f32[32,1,3456]{2,1,0:T(1,128)} async-done(((f32[32,1,3456]{2,1,0:T(1,128)}), f32[32,1,3456]{2,1,0:T(1,128)}, u32[]{:S(2)}, u32[]{:S(2)}) %all-to-all-start.4) | async-done | bytes 442400 | tf_op jit(solution)/shard_map/all_to_all | solution.py:267
  253.7 2.1 reduce.4
  (46 shorter events, 15.4 us)
Async XLA Ops:
  5.8 0.7 copy-start.8
  31.8 38.3 %copy-start.9 = (bf16[9,64,192]{2,1,0:T(8,128)(2,1)S(1)}, bf16[9,64,192]{2,1,0:T(8,128)(2,1)}, u32[]{:S(2)}) copy-start(bf16[9,64,192]{2,1,0:T(8,128)(2,1)} %param.8) | copy-start | bytes 663556
  31.8 51.3 %all-to-all-start.1 = ((bf16[32,128,128]{2,1,0:T(8,128)(2,1)}), bf16[32,128,128]{2,1,0:T(8,128)(2,1)S(1)}, u32[]{:S(2)}, u32[]{:S(2)}) async-start(bf16[32,128,128]{2,1,0:T(8,128)(2,1)} %bitcast.13), calls=%async_computation.1 | async-start | bytes 2097152 | tf_op jit(solution)/shard_map/all_to_all | solution.py:267
  70.7 1.0 copy-start
  71.7 1.0 copy-start.1
  72.7 0.9 copy-start.6
  73.7 0.9 copy-start.7
  130.6 1.0 copy-start.2
  131.6 1.0 copy-start.3
  132.6 0.9 copy-start.4
  133.5 0.9 copy-start.5
  156.7 38.3 %all-to-all-start.3 = ((f32[32,1,3456]{2,1,0:T(1,128)}), f32[32,1,3456]{2,1,0:T(1,128)S(1)}, u32[]{:S(2)}, u32[]{:S(2)}) async-start(f32[32,1,3456]{2,1,0:T(1,128)} %all_to_all.26), calls=%async_computation.3 | async-start | bytes 884736 | tf_op jit(solution)/shard_map/all_to_all | solution.py:267
  175.8 24.6 %copy-start.10 = (bf16[9,64,192]{2,1,0:T(8,128)(2,1)S(1)}, bf16[9,64,192]{2,1,0:T(8,128)(2,1)}, u32[]{:S(2)}) copy-start(bf16[9,64,192]{2,1,0:T(8,128)(2,1)} %param.8) | copy-start | bytes 663556
  194.9 33.1 %all-to-all-start.2 = ((bf16[32,128,128]{2,1,0:T(8,128)(2,1)}), bf16[32,128,128]{2,1,0:T(8,128)(2,1)S(1)}, u32[]{:S(2)}, u32[]{:S(2)}) async-start(bf16[32,128,128]{2,1,0:T(8,128)(2,1)} %bitcast.25), calls=%async_computation.2 | async-start | bytes 2097152 | tf_op jit(solution)/shard_map/all_to_all | solution.py:267
  235.8 17.9 %all-to-all-start.4 = ((f32[32,1,3456]{2,1,0:T(1,128)}), f32[32,1,3456]{2,1,0:T(1,128)}, u32[]{:S(2)}, u32[]{:S(2)}) async-start(f32[32,1,3456]{2,1,0:T(1,128)} %broadcast_in_dim.28), calls=%async_computation.4 | async-start | bytes 884736 | tf_op jit(solution)/shard_map/all_to_all | solution.py:267

commit v3 on v2

--- a/solution.py
+++ b/solution.py
@@ -67,7 +67,14 @@
     )(grid)
 
 
-def stack_kernel(inside_ref, center, left, right, top, bottom, out):
+def stack_kernel(inside_ref, center, *refs):
+    far, (out, left, right, top, bottom, arrived) = refs[:4], refs[-6:]
+    copies = [
+        pltpu.make_async_copy(source, target, arrived.at[i])
+        for i, (source, target) in enumerate(zip(far, (left, right, top, bottom)))
+    ]
+    for copy in copies:
+        copy.start()
     rows_x, _, depth, chans = center.shape
     f32 = jnp.float32
     row = lax.broadcasted_iota(jnp.int32, (depth, chans), 0)
@@ -82,12 +89,17 @@
         return jnp.concatenate([up, t, down], axis=1).astype(jnp.bfloat16)
 
     def plane(x, _):
+        for y in range(CY):
+            out[x + 1, y + 1] = spread(center[x, y])
+
+    def sides(x, _):
         out[x + 1, 0] = spread(left[x], west)
         out[x + 1, CY + 1] = spread(right[x], east)
-        for y in range(CY):
-            out[x + 1, y + 1] = spread(center[x, y])
 
     lax.fori_loop(0, rows_x, plane, None)
+    for copy in copies:
+        copy.wait()
+    lax.fori_loop(0, rows_x, sides, None)
     for at, end, keep in ((0, top, north), (rows_x + 1, bottom, south)):
         out[at, 0] = spread(end[0], keep * west)
         out[at, CY + 1] = spread(end[CY + 1], keep * east)
@@ -95,8 +107,8 @@
             out[at, y] = spread(end[y], keep)
 
 
-def stack_weight_kernel(inside_ref, center, left, right, top, bottom, flat, out, sums):
-    stack_kernel(inside_ref, center, left, right, top, bottom, out)
+def stack_weight_kernel(inside_ref, center, left, right, top, bottom, flat, out, sums, *scratch):
+    stack_kernel(inside_ref, center, left, right, top, bottom, out, *scratch)
     sums[...] = jnp.zeros_like(sums)
     plane_cells = CY * NZ
 
@@ -110,17 +122,26 @@
     lax.fori_loop(0, center.shape[0], plane, None)
 
 
-def stacked_depth(cells, n_narrow, n_region, collective_id, flat=None):
+def stacked_depth(cells, edges, n_narrow, n_region, flat=None):
     rows_x, _, depth, chans = cells.shape
     n, r = lax.axis_index("narrow"), lax.axis_index("region")
     inside = jnp.stack([n > 0, n < n_narrow - 1, r > 0, r < n_region - 1]).astype(jnp.int32)
-    edges = halos(cells, n_narrow, n_region, collective_id)
     stack = jax.ShapeDtypeStruct((rows_x + 2, CY + 2, depth, 3 * chans), cells.dtype)
+    scratch = [pltpu.VMEM(e.shape, e.dtype) for e in edges] + [pltpu.SemaphoreType.DMA((4,))]
     if flat is None:
-        return call(stack_kernel, stack, "svvvvv", "v", [], 40 << 20, inside, cells, *edges)
+        return call(stack_kernel, stack, "svaaaa", "v", scratch, 40 << 20, inside, cells, *edges)
     sums = jax.ShapeDtypeStruct((9, chans, 3 * chans), jnp.float32)
     return call(
-        stack_weight_kernel, (stack, sums), "svvvvvv", "vv", [], 80 << 20, inside, cells, *edges, flat
+        stack_weight_kernel,
+        (stack, sums),
+        "svaaaav",
+        "vv",
+        scratch,
+        80 << 20,
+        inside,
+        cells,
+        *edges,
+        flat,
     )
 
 
@@ -135,32 +156,33 @@
     )
 
 
-def packed(buf, out_ref):
-    rows = out_ref.shape[0]
-
-    def tile(t, _):
-        low = pl.multiple_of(t * TILE, TILE)
-        left = buf[pl.ds(low, TILE), :]
-        right = buf[pl.ds(rows + low, TILE), :]
-        out_ref[pl.ds(low, TILE), :] = jnp.concatenate([left, right], axis=1).astype(jnp.bfloat16)
-
-    lax.fori_loop(0, rows // TILE, tile, None)
-
-
-def unpacked(in_ref, buf):
-    rows, lanes = in_ref.shape
-
-    def tile(t, _):
-        low = pl.multiple_of(t * TILE, TILE)
-        both = in_ref[pl.ds(low, TILE), :].astype(jnp.float32)
-        buf[pl.ds(low, TILE), :] = both[:, : lanes // 2]
-        buf[pl.ds(rows + low, TILE), :] = both[:, lanes // 2 :]
-
-    lax.fori_loop(0, rows // TILE, tile, None)
-
-
-def each_arrival(devices, slots, rows, count_ref, visit):
+def packed(buf, out_ref, half):
+    devices = out_ref.shape[0]
+
+    def block(s, _):
+        low = pl.multiple_of(s * half, half)
+        left = buf[pl.ds(low, half), :]
+        right = buf[pl.ds(devices * half + low, half), :]
+        out_ref[s, pl.ds(0, half), :] = jnp.concatenate([left, right], axis=1).astype(jnp.bfloat16)
+
+    lax.fori_loop(0, devices, block, None)
+
+
+def unpacked(in_ref, buf, half):
+    devices, _, lanes = in_ref.shape
+
+    def block(s, _):
+        low = pl.multiple_of(s * half, half)
+        both = in_ref[s, pl.ds(0, half), :].astype(jnp.float32)
+        buf[pl.ds(low, half), :] = both[:, : lanes // 2]
+        buf[pl.ds(devices * half + low, half), :] = both[:, lanes // 2 :]
+
+    lax.fori_loop(0, devices, block, None)
+
+
+def each_arrival(devices, slots, count_ref, visit):
     half = slots // 2
+    rows = devices * half
 
     def source(s, _):
         here = count_ref[s]
@@ -177,7 +199,7 @@
     lax.fori_loop(0, devices, source, None)
 
 
-def place_kernel(place_ref, vox_ref, rows_ref, out_ref, vox_out_ref, buf):
+def place_kernel(half, place_ref, vox_ref, rows_ref, out_ref, vox_out_ref, buf):
     def group(j, _):
         for u in range(GROUP):
             p = j * GROUP + u
@@ -186,11 +208,11 @@
             vox_out_ref[d] = vox_ref[p]
 
     lax.fori_loop(0, rows_ref.shape[0] // GROUP, group, None)
-    packed(buf, out_ref)
+    packed(buf, out_ref, half)
 
 
 def splat_kernel(devices, slots, vox_ref, count_ref, got_ref, grid_ref, buf, *sums):
-    unpacked(got_ref, buf)
+    unpacked(got_ref, buf, slots // 2)
     voxels, chans = grid_ref.shape
 
     def clear(t, _):
@@ -204,7 +226,7 @@
         each = sums[u % len(sums)]
         each[pl.ds(v, 1), :] += buf[pl.ds(r, 1), :]
 
-    each_arrival(devices, slots, got_ref.shape[0], count_ref, visit)
+    each_arrival(devices, slots, count_ref, visit)
 
     def finish(t, _):
         at = pl.ds(pl.multiple_of(t * TILE, TILE), TILE)
@@ -220,12 +242,12 @@
     def visit(u, k, r):
         buf[pl.ds(r, 1), :] = table_ref[pl.ds(vox_ref[k], 1), :]
 
-    each_arrival(devices, slots, out_ref.shape[0], count_ref, visit)
-    packed(buf, out_ref)
-
-
-def collect_kernel(place_ref, back_ref, out_ref, buf):
-    unpacked(back_ref, buf)
+    each_arrival(devices, slots, count_ref, visit)
+    packed(buf, out_ref, slots // 2)
+
+
+def collect_kernel(half, place_ref, back_ref, out_ref, buf):
+    unpacked(back_ref, buf, half)
 
     def group(j, _):
         for u in range(GROUP):
@@ -236,7 +258,7 @@
 
 
 def call(kernel, out_shape, kinds, out_kinds, scratch, cost, *operands):
-    where = {"s": pltpu.SMEM, "v": pltpu.VMEM}
+    where = {"s": pltpu.SMEM, "v": pltpu.VMEM, "a": pl.ANY}
     specs = [pl.BlockSpec(memory_space=where[k]) for k in out_kinds]
     return pl.pallas_call(
         kernel,
@@ -279,14 +301,20 @@
     voxels = rows_x * CY * NZ
     f32, bf16, i32 = jnp.float32, jnp.bfloat16, jnp.int32
     buffer = pltpu.VMEM((2 * rows, chans), f32)
-    pairs = jax.ShapeDtypeStruct((rows, 2 * chans), bf16)
+    pairs = jax.ShapeDtypeStruct((devices, half, 2 * chans), bf16)
+    spare = 16
+    block = jax.ShapeDtypeStruct((devices, half + spare, 2 * chans), bf16)
+
+    grads = cotangent.reshape(chans, rows_x, CY, NZ).transpose(1, 2, 3, 0)
+    grad_edges = halos(grads, n_narrow, n_region, 0)
+    point_feats, *grad_edges = lax.optimization_barrier((point_feats, *grad_edges))
 
     owner = point_owner[:, 0]
     slot, sent = ranks(owner, devices)
     place = (slot // half) * rows + owner * half + slot % half
     send, send_vox = call(
-        place_kernel,
-        (pairs, jax.ShapeDtypeStruct((2 * rows,), i32)),
+        functools.partial(place_kernel, half),
+        (block, jax.ShapeDtypeStruct((2 * rows,), i32)),
         "ssv",
         "vs",
         [buffer],
@@ -297,8 +325,13 @@
     )
     send_vox = send_vox.reshape(2, devices, half).transpose(1, 0, 2).reshape(devices, slots)
     filled = jnp.arange(slots, dtype=i32)[None, :] < sent[:, None]
-    got_vox = exchanged(jnp.where(filled, send_vox, voxels))
-    got = exchanged(send.reshape(devices, half, 2 * chans)).reshape(rows, 2 * chans)
+    send_vox = jnp.where(filled, send_vox, voxels)
+    digits = jnp.concatenate([send_vox // 128, send_vox % 128], axis=1).astype(bf16)
+    digits = jnp.pad(digits, ((0, 0), (0, spare * 2 * chans - 2 * slots)))
+    digits = digits.reshape(devices, spare, 2 * chans)
+    got = exchanged(lax.dynamic_update_slice(send, digits, (0, half, 0)))
+    digits = got[:, half:].reshape(devices, spare * 2 * chans).astype(i32)
+    got_vox = digits[:, :slots] * 128 + digits[:, slots : 2 * slots]
     count = jnp.sum((got_vox < voxels).astype(i32), axis=1)
     add_at = got_vox.reshape(-1)
     pick_at = jnp.where(got_vox < voxels, got_vox, 0).reshape(-1)
@@ -307,8 +340,8 @@
     backward = w[::-1, ::-1, :, ::-1, :].transpose(0, 1, 3, 2, 4).reshape(3, 3, 3 * chans, chans)
     forward = weight.reshape(3, 3, chans, 3 * chans).transpose(0, 1, 3, 2)
 
-    grads = cotangent.reshape(chans, rows_x, CY, NZ).transpose(1, 2, 3, 0)
-    table = convolved(stacked_depth(grads, n_narrow, n_region, 0), backward).reshape(voxels, chans)
+    grad_stack = stacked_depth(grads, grad_edges, n_narrow, n_region)
+    table = convolved(grad_stack, backward).reshape(voxels, chans)
     picked = call(
         functools.partial(pick_kernel, devices, slots),
         pairs,
@@ -320,7 +353,8 @@
         count,
         table,
     )
-    back = exchanged(picked.reshape(devices, half, 2 * chans)).reshape(rows, 2 * chans)
+    picked, got = lax.optimization_barrier((picked, got))
+    back = exchanged(picked)
 
     grid = call(
         functools.partial(splat_kernel, devices, slots),
@@ -334,8 +368,11 @@
         got,
     )
     cells = grid.reshape(rows_x, CY, NZ, chans)
-    stack, kernels = stacked_depth(cells, n_narrow, n_region, 1, cotangent.reshape(chans, voxels))
+    cell_edges = halos(cells, n_narrow, n_region, 1)
+    flat = cotangent.reshape(chans, voxels)
+    stack, kernels = stacked_depth(cells, cell_edges, n_narrow, n_region, flat)
     total_cells = rows_x * n_region * CY * n_narrow * NZ
+    kernels, back = lax.optimization_barrier((kernels, back))
     parts = exchanged(kernels.reshape(devices, -1))
     mine = jnp.sum(parts, axis=0) * (1.0 / math.sqrt(total_cells))
     back, mine = lax.optimization_barrier((back, mine))
@@ -346,7 +383,7 @@
     conv_out = result.transpose(3, 0, 1, 2).reshape(chans, rows_x, CY * NZ)
 
     point_rows = call(
-        collect_kernel,
+        functools.partial(collect_kernel, half),
         jax.ShapeDtypeStruct((points_here, chans), f32),
         "sv",
         "v",

time: 258 us -> 248 us (0.961)
  blocking collectives: 14.3 us -> 0 us
  starting transfers between devices: 14.6 us -> 24.1 us
  local copies, waits for them, and re-layouts: 26.2 us -> 21.4 us
    all_to_all x1 -> x0, blocking collectives: 14.3 us -> none  [exchanged(): return lax.all_to_all(x, AXES, split_axis=0, concat_axis=0, tiled=True)]
    all_to_all x4, starting transfers between devices: 14.6 us -> 24.1 us  [exchanged(): return lax.all_to_all(x, AXES, split_axis=0, concat_axis=0, tiled=True)]
    unnamed x27 -> x33, local copies, waits for them, and re-layouts: 21.1 us -> 16.8 us
    pallas_call x6, Pallas kernels: 90.2 us -> 94.5 us  [call(): pl.pallas_call(kernel, out_shape=out_shape, in_specs=[pl.BlockSpec(memory...]
  transfers between devices with their start and end apart: 4 -> 4, of which waited for: 2 -> 2; matrix products, arithmetic and copies ran while one was open for 19% -> 17% of each run, Pallas kernels for 22% -> 33%
where the time goes in v3:
time: 248 us; the launch traced here: 247 us
  Pallas kernels  144 us (58%)
  matrix products  34.6 us (14%)
  starting transfers between devices  24.1 us (10%)
  local copies, waits for them, and re-layouts  21.4 us (9%)
  waiting for transfers between devices  16 us (6%)
  other arithmetic  5.37 us (2%)
    pallas_call x6, Pallas kernels, call(): pl.pallas_call(kernel, out_shape=out_shape, in_specs=[pl.BlockSpec(memory...  94.5 us
    pallas_call x2, Pallas kernels, halos(): pl.pallas_call(functools.partial(halo_kernel, n_narrow, n_region), out_sh...  49.7 us
    conv_general_dilated x2, matrix products, convolved(): lax.conv_general_dilated(stack, kernel, (1, 1), 'VALID', dimension_number...  34.2 us
    all_to_all x4, starting transfers between devices, exchanged(): return lax.all_to_all(x, AXES, split_axis=0, concat_axis=0, tiled=True)  24.1 us
    unnamed x33, local copies, waits for them, and re-layouts  16.8 us
    all_to_all x4, waiting for transfers between devices, exchanged(): return lax.all_to_all(x, AXES, split_axis=0, concat_axis=0, tiled=True)  16 us
  transfers between devices with their start and end apart: 4, of which 2 were waited for; matrix products, arithmetic and copies ran while one was open for 17% of the time, Pallas kernels for 33%

profile of v3, /device:TPU:0, one launch (start us, length us, event | category | flops | bytes accessed | tf_op | source)
XLA Modules:
  0.0 246.7 jit_solution(13379073540602395656)
XLA Ops:
  3.2 4.6 %copy.34 = bf16[64,24,512]{0,2,1:T(8,128)(2,1)} copy(bf16[64,24,512]{2,1,0:T(8,128)(2,1)} %param.9) | data formatting | bytes 3145728 | tf_op args[4]
  7.8 24.8 %shard_map.76 = (bf16[24,64,64]{2,1,0:T(8,128)(2,1)}, bf16[24,64,64]{2,1,0:T(8,128)(2,1)}, bf16[10,64,64]{2,1,0:T(8,128)(2,1)}, bf16[10,64,64]{2,1,0:T(8,128)(2,1)}) custom-call(bf16[24,8,64,64]{3,2,1,0:T(8,128)(2,1)} %bitcast.90), custom_call_target="tpu_custom_call" | custom-call | bytes 10485760 | tf_op jit(solution)/shard_map/pallas_call | solution.py:59
  33.5 12.5 %shard_map.77 = (bf16[32,144,128]{2,1,0:T(8,128)(2,1)}, s32[8192]{0:T(1024)S(1)}) custom-call(s32[4096]{0:T(1024)S(1)} %fusion.19.place_ref, s32[4096]{0:T(1024)S(1)} %copy-done.8, f32[4096,64]{1,0:T(8,128)S(1)} %bitcast.83), custom_call_target="tpu_custom_call" | custom-call | bytes 41943040 | tf_op jit(solution)/shard_map/pallas_call | solution.py:263
  46.8 4.5 %all-to-all-start = ((bf16[32,144,128]{2,1,0:T(8,128)(2,1)}), bf16[32,144,128]{2,1,0:T(8,128)(2,1)S(1)}, u32[]{:S(2)}, u32[]{:S(2)}) async-start(bf16[32,144,128]{2,1,0:T(8,128)(2,1)} %constant_dynamic-update-slice_fusion), calls=%async_computation | async-start | bytes 2359296 | tf_op jit(solution)/shard_map/all_to_all | solution.py:289
  52.0 10.9 %shard_map.78 = bf16[26,10,64,192]{3,2,1,0:T(8,128)(2,1)} custom-call(s32[4]{0:T(128)S(1)} %add_convert_fusion.inside_ref, bf16[24,8,64,64]{3,2,1,0:T(8,128)(2,1)} %bitcast.91, bf16[24,64,64]{2,1,0:T(8,128)(2,1)S(1)} %copy-done, bf16[24,64,64]{2,1,0:T(8,128)(2,1)S(1)} %copy-done.1, bf16[10,64,64]{2,1,0:T(8,128)(2,1)S(1)} %copy-done.6, ...), custom_call_target="tpu_custom_call" | custom-call | bytes 41943040 | tf_op jit(solution)/shard_map/pallas_call | solution.py:263
  62.9 16.2 %fusion.27 = f32[24,8,64,64]{3,2,1,0:T(8,128)} fusion(bf16[26,10,64,192]{3,2,1,0:T(8,128)(2,1)} %shard_map.78, bf16[3,3,192,64]{3,2,1,0:T(8,128)(2,1)S(1)} %bitcast.98), kind=kOutput, calls=%fused_computation.61 | convolution fusion | flops 2717908992 | bytes 9756672 | tf_op jit(solution)/shard_map/conv_general_dilated | solution.py:149
  79.1 2.7 %all-to-all-done.got_ref = bf16[32,144,128]{2,1,0:T(8,128)(2,1)S(1)} async-done(((bf16[32,144,128]{2,1,0:T(8,128)(2,1)}), bf16[32,144,128]{2,1,0:T(8,128)(2,1)S(1)}, u32[]{:S(2)}, u32[]{:S(2)}) %all-to-all-start) | async-done | bytes 1179680 | tf_op jit(solution)/shard_map/all_to_all | solution.py:289
  82.0 17.1 %shard_map.79 = bf16[32,128,128]{2,1,0:T(8,128)(2,1)} custom-call(s32[8192]{0:T(1024)S(1)} %bitcast.86, s32[32]{0:T(128)S(1)} %get-tuple-element.65.count_ref, f32[12288,64]{1,0:T(8,128)} %bitcast.93), custom_call_target="tpu_custom_call" | custom-call | bytes 41943040 | tf_op jit(solution)/shard_map/pallas_call | solution.py:263
  99.1 6.9 %all-to-all-start.1 = ((bf16[32,128,128]{2,1,0:T(8,128)(2,1)}), bf16[32,128,128]{2,1,0:T(8,128)(2,1)}, u32[]{:S(2)}, u32[]{:S(2)}) async-start(bf16[32,128,128]{2,1,0:T(8,128)(2,1)} %shard_map.79), calls=%async_computation.1 | async-start | bytes 2097152 | tf_op jit(solution)/shard_map/all_to_all | solution.py:289
  106.0 2.0 copy.47
  108.0 21.9 %shard_map.80 = bf16[12288,64]{1,0:T(8,128)(2,1)} custom-call(s32[8192]{0:T(1024)S(1)} %bitcast.85, s32[32]{0:T(128)S(1)} %get-tuple-element.65.count_ref, bf16[32,144,128]{2,1,0:T(8,128)(2,1)S(1)} %all-to-all-done.got_ref), custom_call_target="tpu_custom_call" | custom-call | bytes 83886080 | tf_op jit(solution)/shard_map/pallas_call | solution.py:263
  129.9 24.8 %shard_map.81 = (bf16[24,64,64]{2,1,0:T(8,128)(2,1)}, bf16[24,64,64]{2,1,0:T(8,128)(2,1)}, bf16[10,64,64]{2,1,0:T(8,128)(2,1)}, bf16[10,64,64]{2,1,0:T(8,128)(2,1)}) custom-call(bf16[24,8,64,64]{3,2,1,0:T(8,128)(2,1)} %bitcast.88), custom_call_target="tpu_custom_call" | custom-call | bytes 10485760 | tf_op jit(solution)/shard_map/pallas_call | solution.py:59
  155.7 1.0 copy-done.3
  158.6 23.3 %shard_map.82 = (bf16[26,10,64,192]{3,2,1,0:T(8,128)(2,1)}, f32[9,64,192]{2,1,0:T(8,128)S(1)}) custom-call(s32[4]{0:T(128)S(1)} %add_convert_fusion.inside_ref, bf16[24,8,64,64]{3,2,1,0:T(8,128)(2,1)} %bitcast.89, bf16[24,64,64]{2,1,0:T(8,128)(2,1)S(1)} %copy-done.2, bf16[24,64,64]{2,1,0:T(8,128)(2,1)S(1)} %copy-done.3, bf16[10,64,64]{2,1,0:T(8,128)(2,1)S(1)} %copy-done.4, ...), custom_call_target="tpu_custom_call" | custom-call | bytes 83886080 | tf_op jit(solution)/shard_map/pallas_call | solution.py:263
  181.9 1.3 all_to_all.21
  183.2 6.8 %all-to-all-start.2 = ((f32[32,1,3456]{2,1,0:T(1,128)}), f32[32,1,3456]{2,1,0:T(1,128)S(1)}, u32[]{:S(2)}, u32[]{:S(2)}) async-start(f32[32,1,3456]{2,1,0:T(1,128)} %all_to_all.21), calls=%async_computation.2 | async-start | bytes 884736 | tf_op jit(solution)/shard_map/all_to_all | solution.py:289
  190.0 18.1 %convolution_convert_fusion = bf16[64,24,8,64]{0,3,2,1:T(8,128)(2,1)} fusion(bf16[26,10,64,192]{3,2,1,0:T(8,128)(2,1)} %get-tuple-element.42, bf16[3,3,64,192]{3,2,1,0:T(8,128)(2,1)S(1)} %bitcast.100), kind=kOutput, calls=%fused_computation | convolution fusion | flops 2718695424 | bytes 8183808 | tf_op jit(solution)/shard_map/conv_general_dilated | solution.py:149
  208.1 4.8 %copy.40 = bf16[64,24,512]{2,1,0:T(8,128)(2,1)} copy(bf16[64,24,512]{0,2,1:T(8,128)(2,1)} %bitcast.94) | data formatting | bytes 3145728
  213.2 8.9 %shard_map.83 = f32[4096,64]{1,0:T(8,128)S(1)} custom-call(s32[4096]{0:T(1024)S(1)} %fusion.19.place_ref, bf16[32,128,128]{2,1,0:T(8,128)(2,1)} %all-to-all-done.1.back_ref), custom_call_target="tpu_custom_call" | custom-call | bytes 41943040 | tf_op jit(solution)/shard_map/pallas_call | solution.py:263
  222.1 1.0 broadcast_in_dim.22
  223.1 5.9 %all-to-all-start.3 = ((f32[32,1,3456]{2,1,0:T(1,128)}), f32[32,1,3456]{2,1,0:T(1,128)}, u32[]{:S(2)}, u32[]{:S(2)}) async-start(f32[32,1,3456]{2,1,0:T(1,128)} %broadcast_in_dim.22), calls=%async_computation.3 | async-start | bytes 884736 | tf_op jit(solution)/shard_map/all_to_all | solution.py:289
  229.1 1.1 copy.41
  230.3 13.3 %all-to-all-done.3 = f32[32,1,3456]{2,1,0:T(1,128)} async-done(((f32[32,1,3456]{2,1,0:T(1,128)}), f32[32,1,3456]{2,1,0:T(1,128)}, u32[]{:S(2)}, u32[]{:S(2)}) %all-to-all-start.3) | async-done | bytes 442400 | tf_op jit(solution)/shard_map/all_to_all | solution.py:289
  243.6 2.1 reduce.3
  (50 shorter events, 9.3 us)
Async XLA Ops:
  3.2 29.4 %copy-start.9 = (bf16[64,4096]{1,0:T(8,128)(2,1)S(1)}, bf16[64,4096]{1,0:T(8,128)(2,1)}, u32[]{:S(2)}) copy-start(bf16[64,4096]{1,0:T(8,128)(2,1)} %param.5) | copy-start | bytes 1572868
  7.8 25.3 %copy-start.11 = (s32[4096,1]{0,1:T(1,128)S(1)}, s32[4096,1]{0,1:T(1,128)}, u32[]{:S(2)}) copy-start(s32[4096,1]{0,1:T(1,128)} %param.6) | copy-start | bytes 49156
  7.8 25.7 %copy-start.8 = (s32[4096]{0:T(1024)S(1)}, s32[4096]{0:T(1024)}, u32[]{:S(2)}) copy-start(s32[4096]{0:T(1024)} %vox_ref.1) | copy-start | bytes 49156
  33.0 18.4 %copy-start.10 = (bf16[9,64,192]{2,1,0:T(8,128)(2,1)S(1)}, bf16[9,64,192]{2,1,0:T(8,128)(2,1)}, u32[]{:S(2)}) copy-start(bf16[9,64,192]{2,1,0:T(8,128)(2,1)} %param.8) | copy-start | bytes 663556
  46.0 6.1 %copy-start = (bf16[24,64,64]{2,1,0:T(8,128)(2,1)S(1)}, bf16[24,64,64]{2,1,0:T(8,128)(2,1)}, u32[]{:S(2)}) copy-start(bf16[24,64,64]{2,1,0:T(8,128)(2,1)} %get-tuple-element.33.refs_0_) | copy-start | bytes 589828
  46.0 6.0 %copy-start.1 = (bf16[24,64,64]{2,1,0:T(8,128)(2,1)S(1)}, bf16[24,64,64]{2,1,0:T(8,128)(2,1)}, u32[]{:S(2)}) copy-start(bf16[24,64,64]{2,1,0:T(8,128)(2,1)} %get-tuple-element.34.refs_1_) | copy-start | bytes 589828
  46.0 6.0 %copy-start.6 = (bf16[10,64,64]{2,1,0:T(8,128)(2,1)S(1)}, bf16[10,64,64]{2,1,0:T(8,128)(2,1)}, u32[]{:S(2)}) copy-start(bf16[10,64,64]{2,1,0:T(8,128)(2,1)} %get-tuple-element.35.refs_2_) | copy-start | bytes 245764
  46.0 6.0 %copy-start.7 = (bf16[10,64,64]{2,1,0:T(8,128)(2,1)S(1)}, bf16[10,64,64]{2,1,0:T(8,128)(2,1)}, u32[]{:S(2)}) copy-start(bf16[10,64,64]{2,1,0:T(8,128)(2,1)} %get-tuple-element.36.refs_3_) | copy-start | bytes 245764
  46.8 34.9 %all-to-all-start = ((bf16[32,144,128]{2,1,0:T(8,128)(2,1)}), bf16[32,144,128]{2,1,0:T(8,128)(2,1)S(1)}, u32[]{:S(2)}, u32[]{:S(2)}) async-start(bf16[32,144,128]{2,1,0:T(8,128)(2,1)} %constant_dynamic-update-slice_fusion), calls=%async_computation | async-start | bytes 2359296 | tf_op jit(solution)/shard_map/all_to_all | solution.py:289
  99.1 82.8 %all-to-all-start.1 = ((bf16[32,128,128]{2,1,0:T(8,128)(2,1)}), bf16[32,128,128]{2,1,0:T(8,128)(2,1)}, u32[]{:S(2)}, u32[]{:S(2)}) async-start(bf16[32,128,128]{2,1,0:T(8,128)(2,1)} %shard_map.79), calls=%async_computation.1 | async-start | bytes 2097152 | tf_op jit(solution)/shard_map/all_to_all | solution.py:289
  154.8 1.0 copy-start.2
  155.7 1.0 copy-start.3
  156.7 0.9 copy-start.4
  157.7 0.9 copy-start.5
  183.2 29.7 %all-to-all-start.2 = ((f32[32,1,3456]{2,1,0:T(1,128)}), f32[32,1,3456]{2,1,0:T(1,128)S(1)}, u32[]{:S(2)}, u32[]{:S(2)}) async-start(f32[32,1,3456]{2,1,0:T(1,128)} %all_to_all.21), calls=%async_computation.2 | async-start | bytes 884736 | tf_op jit(solution)/shard_map/all_to_all | solution.py:289
  223.1 20.5 %all-to-all-start.3 = ((f32[32,1,3456]{2,1,0:T(1,128)}), f32[32,1,3456]{2,1,0:T(1,128)}, u32[]{:S(2)}, u32[]{:S(2)}) async-start(f32[32,1,3456]{2,1,0:T(1,128)} %broadcast_in_dim.22), calls=%async_computation.3 | async-start | bytes 884736 | tf_op jit(solution)/shard_map/all_to_all | solution.py:289

commit v4 on v3

--- a/solution.py
+++ b/solution.py
@@ -15,20 +15,19 @@
 TILE = 512
 
 
-def halo_kernel(n_narrow, n_region, grid, left, right, top, bottom, send, recv):
+def halo_kernel(n_narrow, n_region, faces, ends, left, right, top, bottom, send, recv):
     n, r = lax.axis_index("narrow"), lax.axis_index("region")
     west, east = lax.rem(n + n_narrow - 1, n_narrow), lax.rem(n + 1, n_narrow)
     north, south = lax.rem(r + n_region - 1, n_region), lax.rem(r + 1, n_region)
-    last = grid.shape[0] - 1
     moves = [
-        ((west, r), grid.at[:, 0], right),
-        ((east, r), grid.at[:, CY - 1], left),
-        ((n, north), grid.at[0], bottom.at[pl.ds(1, CY)]),
-        ((n, south), grid.at[last], top.at[pl.ds(1, CY)]),
-        ((west, north), grid.at[0, 0], bottom.at[CY + 1]),
-        ((east, north), grid.at[0, CY - 1], bottom.at[0]),
-        ((west, south), grid.at[last, 0], top.at[CY + 1]),
-        ((east, south), grid.at[last, CY - 1], top.at[0]),
+        ((west, r), faces.at[0], right),
+        ((east, r), faces.at[1], left),
+        ((n, north), ends.at[0], bottom.at[pl.ds(1, CY)]),
+        ((n, south), ends.at[1], top.at[pl.ds(1, CY)]),
+        ((west, north), ends.at[0, 0], bottom.at[CY + 1]),
+        ((east, north), ends.at[0, CY - 1], bottom.at[0]),
+        ((west, south), ends.at[1, 0], top.at[CY + 1]),
+        ((east, south), ends.at[1, CY - 1], top.at[0]),
     ]
     barrier = pltpu.get_barrier_semaphore()
     for device, _, _ in moves:
@@ -53,18 +52,25 @@
 
 def halos(grid, n_narrow, n_region, collective_id):
     rows_x, _, depth, chans = grid.shape
-    side = jax.ShapeDtypeStruct((rows_x, depth, chans), grid.dtype)
-    end = jax.ShapeDtypeStruct((CY + 2, depth, chans), grid.dtype)
+    half = depth // 2
+
+    def paired(cells):
+        return jnp.concatenate([cells[..., :half, :], cells[..., half:, :]], axis=-1)
+
+    faces = paired(jnp.stack([grid[:, 0], grid[:, CY - 1]]))
+    ends = paired(jnp.stack([grid[0], grid[rows_x - 1]]))
+    side = jax.ShapeDtypeStruct((rows_x, half, 2 * chans), grid.dtype)
+    end = jax.ShapeDtypeStruct((CY + 2, half, 2 * chans), grid.dtype)
     anywhere = pl.BlockSpec(memory_space=pl.ANY)
     return pl.pallas_call(
         functools.partial(halo_kernel, n_narrow, n_region),
         out_shape=(side, side, end, end),
-        in_specs=[anywhere],
+        in_specs=[anywhere] * 2,
         out_specs=[anywhere] * 4,
         scratch_shapes=[pltpu.SemaphoreType.DMA((8,)), pltpu.SemaphoreType.DMA((8,))],
         compiler_params=pltpu.CompilerParams(collective_id=collective_id, has_side_effects=True),
         cost_estimate=pl.CostEstimate(flops=0, bytes_accessed=10 << 20, transcendentals=0),
-    )(grid)
+    )(faces, ends)
 
 
 def stack_kernel(inside_ref, center, *refs):
@@ -83,6 +89,7 @@
     def spread(tile, keep=None):
         t = tile.astype(f32)
         if keep is not None:
+            t = jnp.concatenate([t[:, :chans], t[:, chans:]], axis=0)
             t = jnp.where(keep > 0, t, 0.0)
         up = jnp.where(row == 0, 0.0, pltpu.roll(t, 1, 0))
         down = jnp.where(row == depth - 1, 0.0, pltpu.roll(t, depth - 1, 0))
@@ -388,7 +395,7 @@
         "sv",
         "v",
         [buffer],
-        40 << 20,
+        1 << 20,
         place,
         back,
     )

time: 248 us -> 247 us (level)
  Pallas kernels: 144 us -> 129 us
  local copies, waits for them, and re-layouts: 21.4 us -> 35 us
  waiting for transfers between devices: 16 us -> 13.4 us
    pallas_call x2, Pallas kernels: 49.7 us -> 32.2 us  [halos(): pl.pallas_call(functools.partial(halo_kernel, n_narrow, n_region), out_sh...]
    unnamed x33 -> x41, local copies, waits for them, and re-layouts: 16.8 us -> 21.2 us
    concatenate x0 -> x4, other arithmetic: none -> 3.47 us  [paired(): jnp.concatenate([cells[..., :half, :], cells[..., half:, :]], axis=-1)]
    transpose x2, local copies, waits for them, and re-layouts: 0.31 us -> 3.77 us  [shards(): w[::-1, ::-1, :, ::-1, :].transpose(0, 1, 3, 2, 4)]
    all_to_all x4, waiting for transfers between devices: 16 us -> 13.4 us  [exchanged(): return lax.all_to_all(x, AXES, split_axis=0, concat_axis=0, tiled=True)]
  transfers between devices with their start and end apart: 4 -> 4, of which waited for: 2 -> 1; matrix products, arithmetic and copies ran while one was open for 17% -> 21% of each run, Pallas kernels for 33% -> 30%
where the time goes in v4:
time: 247 us; the launch traced here: 246 us
  Pallas kernels  129 us (52%)
  local copies, waits for them, and re-layouts  35 us (14%)
  matrix products  34.6 us (14%)
  starting transfers between devices  24.9 us (10%)
  waiting for transfers between devices  13.4 us (5%)
  other arithmetic  7.83 us (3%)
    pallas_call x6, Pallas kernels, call(): pl.pallas_call(kernel, out_shape=out_shape, in_specs=[pl.BlockSpec(memory...  96.7 us
    conv_general_dilated x2, matrix products, convolved(): lax.conv_general_dilated(stack, kernel, (1, 1), 'VALID', dimension_number...  34.2 us
    pallas_call x2, Pallas kernels, halos(): pl.pallas_call(functools.partial(halo_kernel, n_narrow, n_region), out_sh...  32.2 us
    all_to_all x4, starting transfers between devices, exchanged(): return lax.all_to_all(x, AXES, split_axis=0, concat_axis=0, tiled=True)  24.9 us
    unnamed x41, local copies, waits for them, and re-layouts  21.2 us
    all_to_all x4, waiting for transfers between devices, exchanged(): return lax.all_to_all(x, AXES, split_axis=0, concat_axis=0, tiled=True)  13.4 us
  transfers between devices with their start and end apart: 4, of which 1 were waited for; matrix products, arithmetic and copies ran while one was open for 21% of the time, Pallas kernels for 30%

profile of v4, /device:TPU:0, one launch (start us, length us, event | category | flops | bytes accessed | tf_op | source)
XLA Modules:
  0.0 245.6 jit_solution(7517869736143911331)
XLA Ops:
  0.6 3.4 %copy.42 = bf16[64,24,512]{0,2,1:T(8,128)(2,1)S(1)} copy(bf16[64,24,512]{2,1,0:T(8,128)(2,1)} %param.9) | data formatting | bytes 3145728 | tf_op args[4]
  6.4 15.9 %shard_map.76 = (bf16[24,32,128]{2,1,0:T(8,128)(2,1)}, bf16[24,32,128]{2,1,0:T(8,128)(2,1)}, bf16[10,32,128]{2,1,0:T(8,128)(2,1)}, bf16[10,32,128]{2,1,0:T(8,128)(2,1)}) custom-call(bf16[2,24,32,128]{3,2,1,0:T(8,128)(2,1)} %fusion.7.faces, bf16[2,8,32,128]{3,2,1,0:T(8,128)(2,1)} %fusion.17.ends), custom_call_target="tpu_custom_call" | custom-call | bytes 10485760 | tf_op jit(solution)/shard_map/pallas_call | solution.py:65
  22.3 2.7 %copy.44 = f32[64,4096]{0,1:T(8,128)} copy(bf16[64,4096]{1,0:T(8,128)(2,1)} %param.5) | data formatting | bytes 1572864 | tf_op jit(solution)/shard_map/convert_element_type | solution.py:331
  27.1 12.5 %shard_map.77 = (bf16[32,144,128]{2,1,0:T(8,128)(2,1)}, s32[8192]{0:T(1024)S(1)}) custom-call(s32[4096]{0:T(1024)S(1)} %fusion.27.place_ref, s32[4096]{0:T(1024)S(1)} %copy-done.10, f32[4096,64]{1,0:T(8,128)S(1)} %bitcast.100), custom_call_target="tpu_custom_call" | custom-call | bytes 41943040 | tf_op jit(solution)/shard_map/pallas_call | solution.py:270
  40.4 4.5 %all-to-all-start = ((bf16[32,144,128]{2,1,0:T(8,128)(2,1)}), bf16[32,144,128]{2,1,0:T(8,128)(2,1)}, u32[]{:S(2)}, u32[]{:S(2)}) async-start(bf16[32,144,128]{2,1,0:T(8,128)(2,1)} %constant_dynamic-update-slice_fusion), calls=%async_computation | async-start | bytes 2359296 | tf_op jit(solution)/shard_map/all_to_all | solution.py:296
  45.0 1.9 copy.46
  46.9 1.8 reverse_bitcast_fusion
  48.7 2.0 copy.47
  52.5 11.2 %shard_map.78 = bf16[26,10,64,192]{3,2,1,0:T(8,128)(2,1)} custom-call(s32[4]{0:T(128)S(1)} %add_convert_fusion.inside_ref, bf16[24,8,64,64]{3,2,1,0:T(8,128)(2,1)S(1)} %bitcast.99, bf16[24,32,128]{2,1,0:T(8,128)(2,1)S(1)} %copy-done.4, bf16[24,32,128]{2,1,0:T(8,128)(2,1)S(1)} %copy-done.5, bf16[10,32,128]{2,1,0:T(8,128)(2,1)S(1)} %copy-done.6, ...), custom_call_target="tpu_custom_call" | custom-call | bytes 41943040 | tf_op jit(solution)/shard_map/pallas_call | solution.py:270
  63.8 16.1 %fusion.37 = f32[24,8,64,64]{3,2,1,0:T(8,128)} fusion(bf16[26,10,64,192]{3,2,1,0:T(8,128)(2,1)} %shard_map.78, bf16[3,3,192,64]{3,2,1,0:T(8,128)(2,1)S(1)} %bitcast.117), kind=kOutput, calls=%fused_computation.87 | convolution fusion | flops 2717908992 | bytes 9756672 | tf_op jit(solution)/shard_map/conv_general_dilated | solution.py:156
  81.1 17.3 %shard_map.79 = bf16[32,128,128]{2,1,0:T(8,128)(2,1)} custom-call(s32[8192]{0:T(1024)S(1)} %bitcast.103, s32[32]{0:T(128)S(1)} %get-tuple-element.73.count_ref, f32[12288,64]{1,0:T(8,128)} %bitcast.108), custom_call_target="tpu_custom_call" | custom-call | bytes 41943040 | tf_op jit(solution)/shard_map/pallas_call | solution.py:270
  98.4 8.6 %all-to-all-start.1 = ((bf16[32,128,128]{2,1,0:T(8,128)(2,1)}), bf16[32,128,128]{2,1,0:T(8,128)(2,1)S(1)}, u32[]{:S(2)}, u32[]{:S(2)}) async-start(bf16[32,128,128]{2,1,0:T(8,128)(2,1)} %shard_map.79), calls=%async_computation.1 | async-start | bytes 2097152 | tf_op jit(solution)/shard_map/all_to_all | solution.py:296
  107.0 2.0 copy.59
  109.0 22.3 %shard_map.80 = bf16[12288,64]{1,0:T(8,128)(2,1)} custom-call(s32[8192]{0:T(1024)S(1)} %bitcast.102, s32[32]{0:T(128)S(1)} %get-tuple-element.73.count_ref, bf16[32,144,128]{2,1,0:T(8,128)(2,1)} %all-to-all-done.got_ref), custom_call_target="tpu_custom_call" | custom-call | bytes 83886080 | tf_op jit(solution)/shard_map/pallas_call | solution.py:270
  135.3 16.3 %shard_map.81 = (bf16[24,32,128]{2,1,0:T(8,128)(2,1)}, bf16[24,32,128]{2,1,0:T(8,128)(2,1)}, bf16[10,32,128]{2,1,0:T(8,128)(2,1)}, bf16[10,32,128]{2,1,0:T(8,128)(2,1)}) custom-call(bf16[2,24,32,128]{3,2,1,0:T(8,128)(2,1)} %fusion.6.faces, bf16[2,8,32,128]{3,2,1,0:T(8,128)(2,1)} %fusion.16.ends), custom_call_target="tpu_custom_call" | custom-call | bytes 10485760 | tf_op jit(solution)/shard_map/pallas_call | solution.py:65
  155.3 25.0 %shard_map.82 = (bf16[26,10,64,192]{3,2,1,0:T(8,128)(2,1)}, f32[9,64,192]{2,1,0:T(8,128)S(1)}) custom-call(s32[4]{0:T(128)S(1)} %copy-done.12, bf16[24,8,64,64]{3,2,1,0:T(8,128)(2,1)} %bitcast.106, bf16[24,32,128]{2,1,0:T(8,128)(2,1)S(1)} %copy-done.2, bf16[24,32,128]{2,1,0:T(8,128)(2,1)S(1)} %copy-done.3, bf16[10,32,128]{2,1,0:T(8,128)(2,1)S(1)} %copy-done.8, ...), custom_call_target="tpu_custom_call" | custom-call | bytes 83886080 | tf_op jit(solution)/shard_map/pallas_call | solution.py:270
  181.1 2.4 all_to_all.21
  183.5 5.8 %all-to-all-start.2 = ((f32[32,1,3456]{2,1,0:T(1,128)}), f32[32,1,3456]{2,1,0:T(1,128)S(1)}, u32[]{:S(2)}, u32[]{:S(2)}) async-start(f32[32,1,3456]{2,1,0:T(1,128)} %all_to_all.21), calls=%async_computation.2 | async-start | bytes 884736 | tf_op jit(solution)/shard_map/all_to_all | solution.py:296
  189.3 18.1 %convolution_convert_fusion = bf16[64,24,8,64]{0,3,2,1:T(8,128)(2,1)} fusion(bf16[26,10,64,192]{3,2,1,0:T(8,128)(2,1)} %get-tuple-element.42, bf16[3,3,64,192]{3,2,1,0:T(8,128)(2,1)S(1)} %bitcast.119), kind=kOutput, calls=%fused_computation | convolution fusion | flops 2718695424 | bytes 8183808 | tf_op jit(solution)/shard_map/conv_general_dilated | solution.py:156
  207.4 4.8 %copy.50 = bf16[64,24,512]{2,1,0:T(8,128)(2,1)} copy(bf16[64,24,512]{0,2,1:T(8,128)(2,1)} %bitcast.109) | data formatting | bytes 3145728
  212.5 8.4 %shard_map.83 = f32[4096,64]{1,0:T(8,128)S(1)} custom-call(s32[4096]{0:T(1024)S(1)} %fusion.27.place_ref, bf16[32,128,128]{2,1,0:T(8,128)(2,1)S(1)} %all-to-all-done.1.back_ref), custom_call_target="tpu_custom_call" | custom-call | bytes 1048576 | tf_op jit(solution)/shard_map/pallas_call | solution.py:270
  222.0 5.9 %all-to-all-start.3 = ((f32[32,1,3456]{2,1,0:T(1,128)}), f32[32,1,3456]{2,1,0:T(1,128)}, u32[]{:S(2)}, u32[]{:S(2)}) async-start(f32[32,1,3456]{2,1,0:T(1,128)} %broadcast_in_dim.22), calls=%async_computation.3 | async-start | bytes 884736 | tf_op jit(solution)/shard_map/all_to_all | solution.py:296
  229.2 13.3 %all-to-all-done.3 = f32[32,1,3456]{2,1,0:T(1,128)} async-done(((f32[32,1,3456]{2,1,0:T(1,128)}), f32[32,1,3456]{2,1,0:T(1,128)}, u32[]{:S(2)}, u32[]{:S(2)}) %all-to-all-start.3) | async-done | bytes 442400 | tf_op jit(solution)/shard_map/all_to_all | solution.py:296
  242.5 2.1 reduce.3
  (70 shorter events, 20.2 us)
Async XLA Ops:
  0.6 3.5 %copy-start.15 = (s32[4096,1]{0,1:T(1,128)S(1)}, s32[4096,1]{0,1:T(1,128)}, u32[]{:S(2)}) copy-start(s32[4096,1]{0,1:T(1,128)} %param.6) | copy-start | bytes 49156
  5.4 20.1 %copy-start.10 = (s32[4096]{0:T(1024)S(1)}, s32[4096]{0:T(1024)}, u32[]{:S(2)}) copy-start(s32[4096]{0:T(1024)} %vox_ref.1) | copy-start | bytes 49156
  25.5 1.6 copy-start
  39.6 11.2 %copy-start.4 = (bf16[24,32,128]{2,1,0:T(8,128)(2,1)S(1)}, bf16[24,32,128]{2,1,0:T(8,128)(2,1)}, u32[]{:S(2)}) copy-start(bf16[24,32,128]{2,1,0:T(8,128)(2,1)} %get-tuple-element.33.refs_0_) | copy-start | bytes 589828
  39.6 11.2 %copy-start.5 = (bf16[24,32,128]{2,1,0:T(8,128)(2,1)S(1)}, bf16[24,32,128]{2,1,0:T(8,128)(2,1)}, u32[]{:S(2)}) copy-start(bf16[24,32,128]{2,1,0:T(8,128)(2,1)} %get-tuple-element.34.refs_1_) | copy-start | bytes 589828
  40.4 39.5 %all-to-all-start = ((bf16[32,144,128]{2,1,0:T(8,128)(2,1)}), bf16[32,144,128]{2,1,0:T(8,128)(2,1)}, u32[]{:S(2)}, u32[]{:S(2)}) async-start(bf16[32,144,128]{2,1,0:T(8,128)(2,1)} %constant_dynamic-update-slice_fusion), calls=%async_computation | async-start | bytes 2359296 | tf_op jit(solution)/shard_map/all_to_all | solution.py:296
  50.7 0.9 copy-start.6
  51.6 0.9 copy-start.7
  52.5 11.2 %copy-start.11 = (s32[4]{0:T(128)}, s32[4]{0:T(128)S(1)}, u32[]{:S(2)}) copy-start(s32[4]{0:T(128)S(1)} %add_convert_fusion.inside_ref) | copy-start | bytes 52
  52.5 11.3 %copy-start.13 = (bf16[3,3,3,64,64]{4,3,2,1,0:T(8,128)(2,1)S(1)}, bf16[3,3,3,64,64]{4,3,2,1,0:T(8,128)(2,1)}, u32[]{:S(2)}) copy-start(bf16[3,3,3,64,64]{4,3,2,1,0:T(8,128)(2,1)} %copy.47) | copy-start | bytes 663556
  98.4 82.8 %all-to-all-start.1 = ((bf16[32,128,128]{2,1,0:T(8,128)(2,1)}), bf16[32,128,128]{2,1,0:T(8,128)(2,1)S(1)}, u32[]{:S(2)}, u32[]{:S(2)}) async-start(bf16[32,128,128]{2,1,0:T(8,128)(2,1)} %shard_map.79), calls=%async_computation.1 | async-start | bytes 2097152 | tf_op jit(solution)/shard_map/all_to_all | solution.py:296
  131.3 20.3 %copy-start.12 = (s32[4]{0:T(128)S(1)}, s32[4]{0:T(128)}, u32[]{:S(2)}) copy-start(s32[4]{0:T(128)} %copy-done.11) | copy-start | bytes 52
  151.6 0.9 copy-start.2
  152.6 0.9 copy-start.3
  153.5 0.9 copy-start.8
  154.4 0.9 copy-start.9
  155.3 34.1 %copy-start.14 = (bf16[9,64,192]{2,1,0:T(8,128)(2,1)S(1)}, bf16[9,64,192]{2,1,0:T(8,128)(2,1)}, u32[]{:S(2)}) copy-start(bf16[9,64,192]{2,1,0:T(8,128)(2,1)} %param.8) | copy-start | bytes 663556
  180.3 0.8 copy-start.1
  183.5 28.8 %all-to-all-start.2 = ((f32[32,1,3456]{2,1,0:T(1,128)}), f32[32,1,3456]{2,1,0:T(1,128)S(1)}, u32[]{:S(2)}, u32[]{:S(2)}) async-start(f32[32,1,3456]{2,1,0:T(1,128)} %all_to_all.21), calls=%async_computation.2 | async-start | bytes 884736 | tf_op jit(solution)/shard_map/all_to_all | solution.py:296
  222.0 20.5 %all-to-all-start.3 = ((f32[32,1,3456]{2,1,0:T(1,128)}), f32[32,1,3456]{2,1,0:T(1,128)}, u32[]{:S(2)}, u32[]{:S(2)}) async-start(f32[32,1,3456]{2,1,0:T(1,128)} %broadcast_in_dim.22), calls=%async_computation.3 | async-start | bytes 884736 | tf_op jit(solution)/shard_map/all_to_all | solution.py:296
